TPU v7x, 256 devices: a whole 4x4x8 slice. The times are simulated.
256 devices in a mesh: span: 8 (over z), ha: 8 (over x, core), wa: 4 (over y).
Axes of the slice: x: 4, y: 4, z: 8, core: 2. Of those that a mesh axis runs over, the one named last changes fastest.
Arguments:
- queries: bfloat16 [8, 3, 32, 48, 768], P('span', None, 'ha', 'wa'), may hold values from -5 to 5
- cache_keys: bfloat16 [8, 3, 32, 48, 768], P('span', None, 'ha', 'wa'), may hold values from -5 to 5
- cache_values: bfloat16 [8, 3, 32, 48, 768], P('span', None, 'ha', 'wa'), may hold values from -16 to 16
- grad_attended: bfloat16 [8, 3, 32, 48, 768], P('span', None, 'ha', 'wa'), may hold values from -16 to 16
- radius: int32 [6], replicated, may hold values from 1 to 2, as said below
- frame_count: int32 [8], replicated, may hold values from 1 to 3, as said below
Outputs:
- attended: bfloat16 [8, 3, 32, 48, 768], P('span', None, 'ha', 'wa')
- grad_queries: bfloat16 [8, 3, 32, 48, 768], P('span', None, 'ha', 'wa')
- grad_keys: bfloat16 [8, 3, 32, 48, 768], P('span', None, 'ha', 'wa')
- grad_values: bfloat16 [8, 3, 32, 48, 768], P('span', None, 'ha', 'wa')
Inputs may be any that keep to these rules, and one draw needn't show every extreme that they name: Some head has radius 2 and some other head has radius 1. Frame slots of block c at or past frame_count[c] hold padding; some block has all 3 slots live.
All inputs are finite; a program needn't handle non-finite values.
Results may differ from a plain program's by a relative error of at most 0.02.
Values may be sent and summed in bfloat16 or wider, within the bound.
A program may use at most 128 MiB of HBM per device.

v0:
```python
import math

import jax
import jax.numpy as jnp
from jax import lax
from jax.sharding import PartitionSpec as P

RMAX = 2


def padded(block, sides, width):
    for axis, dim in sides:
        count = lax.axis_size(axis)
        forward = [(i, i + 1) for i in range(count - 1)]
        backward = [(target, source) for source, target in forward]
        low = lax.ppermute(
            lax.slice_in_dim(block, block.shape[dim] - width, None, axis=dim), axis, forward
        )
        high = lax.ppermute(lax.slice_in_dim(block, 0, width, axis=dim), axis, backward)
        block = jnp.concatenate([low, block, high], axis=dim)
    return block


def near_table(radius, tile_h, tile_w, margin, first_row, first_col, full_h, full_w):
    rows_local = jnp.arange(tile_h)
    rows_wide = jnp.arange(tile_h + 2 * margin) - margin
    cols_local = jnp.arange(tile_w)
    cols_wide = jnp.arange(tile_w + 2 * margin) - margin
    gap_rows = jnp.abs(rows_local[:, None] - rows_wide[None, :])
    gap_cols = jnp.abs(cols_local[:, None] - cols_wide[None, :])
    inside_rows = (first_row + rows_wide >= 0) & (first_row + rows_wide < full_h)
    inside_cols = (first_col + cols_wide >= 0) & (first_col + cols_wide < full_w)
    reach = jnp.maximum(gap_rows[:, None, :, None], gap_cols[None, :, None, :])
    inside = inside_rows[:, None] & inside_cols[None, :]
    within = (reach[None] <= radius[:, None, None, None, None]) & inside[None, None, None]
    return within.reshape(
        radius.shape[0], tile_h * tile_w, (tile_h + 2 * margin) * (tile_w + 2 * margin)
    )


def with_frames(spatial, frame_live):
    heads, rows, columns = spatial.shape
    frames = frame_live.shape[0]
    joined = spatial[:, None, :, None, :] & frame_live[None, None, None, :, None]
    joined = jnp.broadcast_to(joined, (heads, frames, rows, frames, columns))
    return joined.reshape(heads, frames * rows, frames * columns)


def live_frames(frame_count, block_id, frames):
    picked = jnp.arange(frame_count.shape[0]) == block_id
    count = jnp.sum(jnp.where(picked, frame_count, 0))
    return jnp.arange(frames) < count


def over_tiles(advance, carried, piece):
    block_ids = jnp.arange(piece.shape[0], dtype=jnp.int32)

    def inner(current, item):
        return (advance(current, item[0], item[1]), None)

    result, _ = lax.scan(inner, carried, (piece, block_ids))
    return result


def shards(queries, cache_keys, cache_values, grad_attended, radius, frame_count):
    frames, tile_h, tile_w, width = queries.shape[1:]
    heads = radius.shape[0]
    depth = width // heads
    margin = RMAX
    scale = 1.0 / math.sqrt(depth)
    own_block = lax.axis_index("span")
    block_total = lax.axis_size("span")
    first_row = lax.axis_index("ha") * tile_h
    first_col = lax.axis_index("wa") * tile_w
    spatial = near_table(
        radius,
        tile_h,
        tile_w,
        margin,
        first_row,
        first_col,
        tile_h * lax.axis_size("ha"),
        tile_w * lax.axis_size("wa"),
    )
    local_rows = frames * tile_h * tile_w
    wide_rows = frames * (tile_h + 2 * margin) * (tile_w + 2 * margin)
    query_rows = queries.reshape(local_rows, heads, depth)
    key_local = cache_keys.reshape(local_rows, heads, depth)
    value_local = cache_values.reshape(local_rows, heads, depth)
    upstream = grad_attended.reshape(local_rows, heads, depth)
    key_mask = with_frames(
        jnp.transpose(spatial, (0, 2, 1)), live_frames(frame_count, own_block, frames)
    )
    bundle = jnp.concatenate([cache_keys, cache_values, queries, grad_attended], axis=4)

    def forward_step(carried, tile, block_id):

        def forward_run(current):
            top, total, accum = current
            key_rows = tile[..., :width].reshape(wide_rows, heads, depth)
            value_rows = tile[..., width : 2 * width].reshape(wide_rows, heads, depth)
            allowed = with_frames(spatial, live_frames(frame_count, block_id, frames))
            score = (
                jnp.einsum("qhd,khd->hqk", query_rows, key_rows, preferred_element_type=jnp.float32)
                * scale
            )
            score = jnp.where(allowed, score, -jnp.inf)
            new_top = jnp.maximum(top, jnp.max(score, axis=2))
            weight = jnp.exp(score - new_top[:, :, None])
            fading = jnp.exp(top - new_top)
            total = total * fading + jnp.sum(weight, axis=2)
            accum = accum * fading[:, :, None] + jnp.einsum(
                "hqk,khd->hqd",
                weight.astype(jnp.bfloat16),
                value_rows,
                preferred_element_type=jnp.float32,
            )
            return (new_top, total, accum)

        active = (block_id >= 0) & (block_id <= own_block)
        return lax.cond(active, forward_run, lambda current: current, carried)

    def query_grad_step(carried, tile, block_id):

        def query_run(current):
            key_rows = tile[..., :width].reshape(wide_rows, heads, depth)
            value_rows = tile[..., width : 2 * width].reshape(wide_rows, heads, depth)
            allowed = with_frames(spatial, live_frames(frame_count, block_id, frames))
            score = (
                jnp.einsum("qhd,khd->hqk", query_rows, key_rows, preferred_element_type=jnp.float32)
                * scale
            )
            prob = jnp.exp(jnp.where(allowed, score - log_total[:, :, None], -jnp.inf))
            push = jnp.einsum(
                "qhd,khd->hqk", upstream, value_rows, preferred_element_type=jnp.float32
            )
            slope = (prob * (push - delta[:, :, None])).astype(jnp.bfloat16)
            return current + jnp.einsum(
                "hqk,khd->hqd", slope, key_rows, preferred_element_type=jnp.float32
            )

        active = (block_id >= 0) & (block_id <= own_block)
        return lax.cond(active, query_run, lambda current: current, carried)

    def key_grad_step(carried, tile, block_id):

        def key_run(current):
            grad_k, grad_v = current
            asking = tile[..., -2 * width : -width].reshape(wide_rows, heads, depth)
            asking_grad = tile[..., -width:].reshape(wide_rows, heads, depth)
            stat_tile = lax.dynamic_index_in_dim(
                stats_all, jnp.clip(block_id, 0, block_total - 1), 0, keepdims=False
            )
            stat_rows = stat_tile.reshape(wide_rows, 2 * heads)
            row_lse = jnp.transpose(stat_rows[:, :heads])
            row_delta = jnp.transpose(stat_rows[:, heads:])
            score = (
                jnp.einsum("qhd,khd->hqk", asking, key_local, preferred_element_type=jnp.float32)
                * scale
            )
            prob = jnp.exp(jnp.where(key_mask, score - row_lse[:, :, None], -jnp.inf))
            grad_v = grad_v + jnp.einsum(
                "hqk,qhd->khd",
                prob.astype(jnp.bfloat16),
                asking_grad,
                preferred_element_type=jnp.float32,
            )
            push = jnp.einsum(
                "qhd,khd->hqk", asking_grad, value_local, preferred_element_type=jnp.float32
            )
            slope = (prob * (push - row_delta[:, :, None])).astype(jnp.bfloat16)
            grad_k = grad_k + jnp.einsum(
                "hqk,qhd->khd", slope, asking, preferred_element_type=jnp.float32
            )
            return (grad_k, grad_v)

        active = (block_id >= own_block) & (block_id < block_total)
        return lax.cond(active, key_run, lambda current: current, carried)

    start_state = (
        jnp.full((heads, local_rows), -jnp.inf, jnp.float32),
        jnp.zeros((heads, local_rows), jnp.float32),
        jnp.zeros((heads, local_rows, depth), jnp.float32),
    )
    everything = lax.all_gather(bundle, "span", axis=0, tiled=True)
    wide_all = padded(everything, (("ha", 2), ("wa", 3)), RMAX)
    top, total, accum = over_tiles(forward_step, start_state, wide_all)
    attended_rows = jnp.transpose((accum / total[:, :, None]).astype(jnp.bfloat16), (1, 0, 2))
    log_total = top + jnp.log(total)
    delta = jnp.einsum("qhd,qhd->hq", upstream, attended_rows, preferred_element_type=jnp.float32)
    stats = jnp.concatenate([jnp.transpose(log_total), jnp.transpose(delta)], axis=1)
    stats = stats.reshape(1, frames, tile_h, tile_w, 2 * heads)
    stat_wide = padded(stats, (("ha", 2), ("wa", 3)), RMAX)
    stats_all = lax.all_gather(stat_wide, "span", axis=0, tiled=True)
    query_start = jnp.zeros((heads, local_rows, depth), jnp.float32)
    key_start = (
        jnp.zeros((local_rows, heads, depth), jnp.float32),
        jnp.zeros((local_rows, heads, depth), jnp.float32),
    )
    grad_q = over_tiles(query_grad_step, query_start, wide_all)
    grad_k, grad_v = over_tiles(key_grad_step, key_start, wide_all)
    final = (1, frames, tile_h, tile_w, width)
    attended = attended_rows.reshape(final)
    grad_queries = jnp.transpose(grad_q * scale, (1, 0, 2)).astype(jnp.bfloat16).reshape(final)
    grad_keys = (grad_k * scale).astype(jnp.bfloat16).reshape(final)
    grad_values = grad_v.astype(jnp.bfloat16).reshape(final)
    return (attended, grad_queries, grad_keys, grad_values)


def solution(mesh):
    placed = (
        P("span", None, "ha", "wa", None),
        P("span", None, "ha", "wa", None),
        P("span", None, "ha", "wa", None),
        P("span", None, "ha", "wa", None),
        P(),
        P(),
    )
    return jax.shard_map(
        shards,
        mesh=mesh,
        in_specs=placed,
        out_specs=(
            P("span", None, "ha", "wa", None),
            P("span", None, "ha", "wa", None),
            P("span", None, "ha", "wa", None),
            P("span", None, "ha", "wa", None),
        ),
        check_vma=False,
    )
```

profile of v0, /device:TPU:2, one launch (start us, length us, event | category | flops | bytes accessed | tf_op | source)
XLA Modules:
  0.0 647.1 jit_solution(17913290227682815183)
XLA Ops:
  7.2 2.6 pad_maximum_fusion.4
  9.8 84.9 %all-gather.2.cloned.1.call-done = bf16[8,3,4,12,3072]{4,2,3,1,0:T(4,128)(2,1)} async-done(((bf16[1,3,4,12,3072]{4,2,3,1,0:T(4,128)(2,1)}), bf16[8,3,4,12,3072]{4,2,3,1,0:T(4,128)(2,1)}) %all-gather.2.cloned.1.call-update) | async-done | bytes 7077904 | tf_op jit(solution)/shard_map/all_gather | solution.py:185
  94.7 9.5 %fusion.57 = (bf16[8,3,2,12,3072]{4,2,3,1,0:T(2,128)(2,1)S(1)}, bf16[8,3,2,12,3072]{4,2,3,1,0:T(2,128)(2,1)S(1)}) fusion(bf16[8,3,4,12,3072]{4,2,3,1,0:T(4,128)(2,1)} %all-gather.2.cloned.1.call-done), kind=kLoop, calls=%fused_computation.100 | loop fusion | bytes 14155776 | tf_op jit(solution)/shard_map/slice | solution.py:17
  108.2 3.8 copy.86
  112.0 4.1 collective-permute-start.1
  116.0 33.0 %collective-permute-done = bf16[8,3,2,12,3072]{4,0,3,2,1:T(8,128)(2,1)S(1)} collective-permute-done((bf16[8,3,2,12,3072]{4,0,3,2,1:T(8,128)(2,1)S(1)}, bf16[8,3,2,12,3072]{4,0,3,2,1:T(8,128)(2,1)S(1)}, u32[]{:S(2)}, u32[]{:S(2)}) %collective-permute-start) | collective-permute-done | bytes 3538976 | tf_op jit(solution)/shard_map/ppermute | solution.py:16
  149.0 3.6 copy.87
  152.7 2.5 collective-permute-done.1
  155.2 5.6 copy.88
  160.9 5.3 pad_maximum_fusion.3
  166.2 4.8 collective-permute-start.2
  198.1 22.7 %collective-permute-done.2 = bf16[8,3,8,2,3072]{4,2,3,1,0:T(8,128)(2,1)} collective-permute-done((bf16[8,3,8,2,3072]{4,2,3,1,0:T(8,128)(2,1)}, bf16[8,3,8,2,3072]{4,2,3,1,0:T(8,128)(2,1)}, u32[]{:S(2)}, u32[]{:S(2)}) %collective-permute-start.2) | collective-permute-done | bytes 2359328 | tf_op jit(solution)/shard_map/ppermute | solution.py:16
  220.7 6.0 collective-permute-done.3
  226.8 13.9 %pad_maximum_fusion = bf16[8,3,8,16,3072]{4,2,3,1,0:T(8,128)(2,1)S(1)} fusion(bf16[8,3,8,2,3072]{4,2,3,1,0:T(8,128)(2,1)} %collective-permute-done.3, bf16[8,3,2,12,3072]{4,2,3,1,0:T(2,128)(2,1)} %copy-done, bf16[8,3,4,12,3072]{4,2,3,1,0:T(4,128)(2,1)} %all-gather.2.cloned.1.call-done, bf16[8,3,2,12,3072]{4,2,3,1,0:T(2,128)(2,1)S(1)} %copy.87, ...), kind=kLoop, calls=%fused_computation.67 | loop fusion | flops 94371840 | bytes 37748736 | tf_op jit(solution)/shard_map/concatenate | solution.py:20
  240.7 12.6 %copy.90 = bf16[8,3,8,16,3072]{4,3,2,1,0:T(8,128)(2,1)} copy(bf16[8,3,8,16,3072]{4,2,3,1,0:T(8,128)(2,1)S(1)} %pad_maximum_fusion) | data formatting | bytes 37748736
  253.4 26.6 %while.42 = (s32[]{:T(128)}, f32[6,144]{1,0:T(8,128)S(1)}, f32[6,144]{1,0:T(8,128)S(1)}, f32[6,144,128]{2,1,0:T(8,128)S(1)}, s32[8]{0:T(128)S(1)}, /*index=5*/s3...) while((s32[]{:T(128)}, f32[6,144]{1,0:T(8,128)S(1)}, ...), condition=%wide.region_6.7_spmd.clone, body=%wide.region_0.6_spmd.clone.sunk | while | flops 172599008 | bytes 17480200 | solution.py:61
  255.3 11.1 %conditional.9 = ((f32[6,144]{1,0:T(8,128)S(1)}, f32[6,144]{1,0:T(8,128)S(1)}, f32[6,144,128]{2,1,0:T(8,128)S(1)})) conditional(s32[]{:T(128)} %convert_element_type.76, (f32[6,144]{1,0:T(8,128)S(1)}, f32[6,144]{1,0:T(8,128)S(1)}, f32[6,144,128]{2,1,0:T(8,128)S(1)}) %tuple.115, (s32[4,12,8,16]{3,2,1,0:T(8,128)S(1)}, s32[]{:T(128)}, s32[8]{0:T(128)}, ...), branch_computations={%region_1.1_spmd, %region_2.0_spmd} | conditional | flops 172599008 | bytes 17479918 | solution.py:121
  285.1 3.6 collective-permute-start.5
  290.0 29.6 %while.43 = (s32[]{:T(128)}, f32[6,144,128]{2,1,0:T(8,128)}, s32[8]{0:T(128)}, s32[]{:T(128)}, s32[8]{0:T(128)}, /*index=5*/bf16[8,3,8,16,3072]{4,3,2,1,0:T(8,12...) while((s32[]{:T(128)}, f32[6,144,128]{2,1,0:T(8,128)}, ...), condition=%wide.region_11.12_spmd.clone, body=%wide.region_7.11_spmd.clone.sunk | while | flops 257089568 | bytes 18095392 | solution.py:61
  292.3 11.0 %conditional.10 = (f32[6,144,128]{2,1,0:T(8,128)}) conditional(s32[]{:T(128)} %convert_element_type.77, f32[6,144,128]{2,1,0:T(8,128)} %get-tuple-element.945, (s32[4,12,8,16]{3,2,1,0:T(8,128)S(1)}, s32[]{:T(128)}, s32[8]{0:T(128)}, bf16[8,3,8,16,3072]{4,3,2,1,0:T(8,128)(2,1)}, s32[]{:T(128)}, /*index=5*/bf16[144,6,128]{2,0,1:T(8,128)(2,1)}, ...), branch_computations={%region_8.8_spmd, %region_9.10_spmd} | conditional | flops 257089568 | bytes 18095118 | solution.py:143
  300.7 2.7 fusion.23
  327.4 2.8 collective-permute-done.7
  331.3 180.3 %all_gather.7 = f32[8,3,8,16,12]{3,2,4,1,0:T(8,128)S(1)} all-gather(f32[1,3,8,16,12]{3,2,4,1,0:T(8,128)S(1)} %copy.99), channel_id=1, replica_groups=mesh['span'=8,'ha'=8,'wa'=4] {'span'}, dimensions={0}, use_global_device_ids=true | all-gather | bytes 165888 | tf_op jit(solution)/shard_map/all_gather | solution.py:194
  513.5 122.9 %while.44 = (s32[]{:T(128)}, f32[144,6,128]{2,0,1:T(8,128)S(1)}, f32[144,6,128]{2,0,1:T(8,128)}, s32[8]{0:T(128)S(1)}, s32[]{:T(128)}, /*index=5*/bf16[8,3,8,16,...) while((s32[]{:T(128)}, f32[144,6,128]{2,0,1:T(8,128)S(1)}, ...), condition=%wide.region_16.17_spmd.clone, body=%wide.region_13.16_spmd.clone.sunk | while | flops 342282240 | bytes 23095652 | solution.py:61
  515.4 13.5 %conditional.11 = ((f32[144,6,128]{2,0,1:T(8,128)S(1)}, f32[144,6,128]{2,0,1:T(8,128)})) conditional(s32[]{:T(128)} %convert_element_type.78, (f32[144,6,128]{2,0,1:T(8,128)S(1)}, f32[144,6,128]{2,0,1:T(8,128)}) %tuple.120, (bf16[8,3,8,16,3072]{4,3,2,1,0:T(8,128)(2,1)}, s32[]{:T(128)}, bf16[144,6,128]{2,0,1:T(8,128)(2,1)}, s32[]{:T(128)}, ...), branch_computations={%region_14.14_spmd, %region_15.15_spmd} | conditional | flops 342282240 | bytes 23095408 | solution.py:178
  524.1 2.6 fusion.40
  526.6 2.2 fusion.41
  530.8 13.5 %conditional.11 = ((f32[144,6,128]{2,0,1:T(8,128)S(1)}, f32[144,6,128]{2,0,1:T(8,128)})) conditional(s32[]{:T(128)} %convert_element_type.78, (f32[144,6,128]{2,0,1:T(8,128)S(1)}, f32[144,6,128]{2,0,1:T(8,128)}) %tuple.120, (bf16[8,3,8,16,3072]{4,3,2,1,0:T(8,128)(2,1)}, s32[]{:T(128)}, bf16[144,6,128]{2,0,1:T(8,128)(2,1)}, s32[]{:T(128)}, ...), branch_computations={%region_14.14_spmd, %region_15.15_spmd} | conditional | flops 342282240 | bytes 23095408 | solution.py:178
  539.4 2.6 fusion.40
  542.0 2.2 fusion.41
  546.1 13.5 %conditional.11 = ((f32[144,6,128]{2,0,1:T(8,128)S(1)}, f32[144,6,128]{2,0,1:T(8,128)})) conditional(s32[]{:T(128)} %convert_element_type.78, (f32[144,6,128]{2,0,1:T(8,128)S(1)}, f32[144,6,128]{2,0,1:T(8,128)}) %tuple.120, (bf16[8,3,8,16,3072]{4,3,2,1,0:T(8,128)(2,1)}, s32[]{:T(128)}, bf16[144,6,128]{2,0,1:T(8,128)(2,1)}, s32[]{:T(128)}, ...), branch_computations={%region_14.14_spmd, %region_15.15_spmd} | conditional | flops 342282240 | bytes 23095408 | solution.py:178
  554.8 2.6 fusion.40
  557.4 2.2 fusion.41
  561.5 13.5 %conditional.11 = ((f32[144,6,128]{2,0,1:T(8,128)S(1)}, f32[144,6,128]{2,0,1:T(8,128)})) conditional(s32[]{:T(128)} %convert_element_type.78, (f32[144,6,128]{2,0,1:T(8,128)S(1)}, f32[144,6,128]{2,0,1:T(8,128)}) %tuple.120, (bf16[8,3,8,16,3072]{4,3,2,1,0:T(8,128)(2,1)}, s32[]{:T(128)}, bf16[144,6,128]{2,0,1:T(8,128)(2,1)}, s32[]{:T(128)}, ...), branch_computations={%region_14.14_spmd, %region_15.15_spmd} | conditional | flops 342282240 | bytes 23095408 | solution.py:178
  570.2 2.6 fusion.40
  572.7 2.2 fusion.41
  576.8 13.5 %conditional.11 = ((f32[144,6,128]{2,0,1:T(8,128)S(1)}, f32[144,6,128]{2,0,1:T(8,128)})) conditional(s32[]{:T(128)} %convert_element_type.78, (f32[144,6,128]{2,0,1:T(8,128)S(1)}, f32[144,6,128]{2,0,1:T(8,128)}) %tuple.120, (bf16[8,3,8,16,3072]{4,3,2,1,0:T(8,128)(2,1)}, s32[]{:T(128)}, bf16[144,6,128]{2,0,1:T(8,128)(2,1)}, s32[]{:T(128)}, ...), branch_computations={%region_14.14_spmd, %region_15.15_spmd} | conditional | flops 342282240 | bytes 23095408 | solution.py:178
  585.5 2.6 fusion.40
  588.1 2.2 fusion.41
  592.2 13.5 %conditional.11 = ((f32[144,6,128]{2,0,1:T(8,128)S(1)}, f32[144,6,128]{2,0,1:T(8,128)})) conditional(s32[]{:T(128)} %convert_element_type.78, (f32[144,6,128]{2,0,1:T(8,128)S(1)}, f32[144,6,128]{2,0,1:T(8,128)}) %tuple.120, (bf16[8,3,8,16,3072]{4,3,2,1,0:T(8,128)(2,1)}, s32[]{:T(128)}, bf16[144,6,128]{2,0,1:T(8,128)(2,1)}, s32[]{:T(128)}, ...), branch_computations={%region_14.14_spmd, %region_15.15_spmd} | conditional | flops 342282240 | bytes 23095408 | solution.py:178
  600.9 2.6 fusion.40
  603.5 2.2 fusion.41
  607.6 13.5 %conditional.11 = ((f32[144,6,128]{2,0,1:T(8,128)S(1)}, f32[144,6,128]{2,0,1:T(8,128)})) conditional(s32[]{:T(128)} %convert_element_type.78, (f32[144,6,128]{2,0,1:T(8,128)S(1)}, f32[144,6,128]{2,0,1:T(8,128)}) %tuple.120, (bf16[8,3,8,16,3072]{4,3,2,1,0:T(8,128)(2,1)}, s32[]{:T(128)}, bf16[144,6,128]{2,0,1:T(8,128)(2,1)}, s32[]{:T(128)}, ...), branch_computations={%region_14.14_spmd, %region_15.15_spmd} | conditional | flops 342282240 | bytes 23095408 | solution.py:178
  616.3 2.6 fusion.40
  618.8 2.2 fusion.41
  622.9 13.5 %conditional.11 = ((f32[144,6,128]{2,0,1:T(8,128)S(1)}, f32[144,6,128]{2,0,1:T(8,128)})) conditional(s32[]{:T(128)} %convert_element_type.78, (f32[144,6,128]{2,0,1:T(8,128)S(1)}, f32[144,6,128]{2,0,1:T(8,128)}) %tuple.120, (bf16[8,3,8,16,3072]{4,3,2,1,0:T(8,128)(2,1)}, s32[]{:T(128)}, bf16[144,6,128]{2,0,1:T(8,128)(2,1)}, s32[]{:T(128)}, ...), branch_computations={%region_14.14_spmd, %region_15.15_spmd} | conditional | flops 342282240 | bytes 23095408 | solution.py:178
  631.6 2.6 fusion.40
  634.2 2.2 fusion.41
  (283 shorter events, 153.1 us)
Async XLA Ops:
  7.2 87.6 %all-gather.2.cloned.1.call-start = ((), (), s32[]{:S(2)}) async-start(), calls=%async_computation | async-start | bytes 7962624 | tf_op jit(solution)/shard_map/all_gather | solution.py:185
  106.2 42.8 %collective-permute-start = (bf16[8,3,2,12,3072]{4,0,3,2,1:T(8,128)(2,1)S(1)}, bf16[8,3,2,12,3072]{4,0,3,2,1:T(8,128)(2,1)S(1)}, u32[]{:S(2)}, u32[]{:S(2)}) collective-permute-start(bf16[8,3,2,12,3072]{4,0,3,2,1:T(8,128)(2,1)S(1)} %copy.85), channel_id=1, source_target_pairs={{0,4},{4,8},{8,12},{12,16},{16,20},{20,24},{24,28},{1,5},{5,9},{9,... | collective-permute-start | bytes 10616840 | tf_op jit(solution)/shard_map/ppermute | solution.py:16
  108.1 52.7 %slice-start = ((s8[7077888]{0:T(1024)(128)(4,1)}), s8[4194304]{0:T(1024)(128)(4,1)S(1)}, s32[]{:S(2)}) async-start(s8[7077888]{0:T(1024)(128)(4,1)} %bitcast.91), calls=%async_computation.1 | async-start | bytes 8388608
  112.0 48.9 %slice-start.1 = ((s8[7077888]{0:T(1024)(128)(4,1)}), s8[2883584]{0:T(1024)(128)(4,1)S(1)}, s32[]{:S(2)}) async-start(s8[7077888]{0:T(1024)(128)(4,1)} %bitcast.91), calls=%async_computation.2 | async-start | bytes 5767168
  112.0 43.2 %collective-permute-start.1 = (bf16[8,3,2,12,3072]{4,0,3,2,1:T(8,128)(2,1)}, bf16[8,3,2,12,3072]{4,0,3,2,1:T(8,128)(2,1)}, u32[]{:S(2)}, u32[]{:S(2)}) collective-permute-start(bf16[8,3,2,12,3072]{4,0,3,2,1:T(8,128)(2,1)} %copy.86), channel_id=1, source_target_pairs={{4,0},{8,4},{12,8},{16,12},{20,16},{24,20},{28,24},{5,1},{9,5},{13... | collective-permute-start | bytes 10616840 | tf_op jit(solution)/shard_map/ppermute | solution.py:19
  160.8 5.3 copy-start
  160.8 11.6 %copy-start.5 = (bf16[1,3,4,12,768]{4,2,3,1,0:T(4,128)(2,1)S(1)}, bf16[1,3,4,12,768]{4,2,3,1,0:T(4,128)(2,1)}, u32[]{:S(2)}) copy-start(bf16[1,3,4,12,768]{4,2,3,1,0:T(4,128)(2,1)} %param.18) | copy-start | bytes 663556
  160.9 12.4 %copy-start.6 = (bf16[1,3,4,12,768]{4,2,3,1,0:T(4,128)(2,1)S(1)}, bf16[1,3,4,12,768]{4,2,3,1,0:T(4,128)(2,1)}, u32[]{:S(2)}) copy-start(bf16[1,3,4,12,768]{4,2,3,1,0:T(4,128)(2,1)} %param.21) | copy-start | bytes 663556
  160.9 13.1 %copy-start.7 = (bf16[1,3,4,12,768]{4,2,3,1,0:T(4,128)(2,1)S(1)}, bf16[1,3,4,12,768]{4,2,3,1,0:T(4,128)(2,1)}, u32[]{:S(2)}) copy-start(bf16[1,3,4,12,768]{4,2,3,1,0:T(4,128)(2,1)} %param.19) | copy-start | bytes 663556
  160.9 13.8 %copy-start.8 = (bf16[1,3,4,12,768]{4,2,3,1,0:T(4,128)(2,1)S(1)}, bf16[1,3,4,12,768]{4,2,3,1,0:T(4,128)(2,1)}, u32[]{:S(2)}) copy-start(bf16[1,3,4,12,768]{4,2,3,1,0:T(4,128)(2,1)} %param.20) | copy-start | bytes 663556
  166.2 54.5 %collective-permute-start.2 = (bf16[8,3,8,2,3072]{4,2,3,1,0:T(8,128)(2,1)}, bf16[8,3,8,2,3072]{4,2,3,1,0:T(8,128)(2,1)}, u32[]{:S(2)}, u32[]{:S(2)}) collective-permute-start(bf16[8,3,8,2,3072]{4,2,3,1,0:T(8,128)(2,1)} %get-tuple-element.644), channel_id=1, source_target_pairs={{0,1},{1,2},{2,3},{4,5},{5,6},{6,7},{8,9},{9,10},{10,11},{12,13},{... | collective-permute-start | bytes 7077896 | tf_op jit(solution)/shard_map/ppermute | solution.py:16
  170.9 55.8 %collective-permute-start.3 = (bf16[8,3,8,2,3072]{4,2,3,1,0:T(8,128)(2,1)}, bf16[8,3,8,2,3072]{4,2,3,1,0:T(8,128)(2,1)}, u32[]{:S(2)}, u32[]{:S(2)}) collective-permute-start(bf16[8,3,8,2,3072]{4,2,3,1,0:T(8,128)(2,1)} %get-tuple-element.645), channel_id=1, source_target_pairs={{1,0},{2,1},{3,2},{5,4},{6,5},{7,6},{9,8},{10,9},{11,10},{13,12},{... | collective-permute-start | bytes 7077896 | tf_op jit(solution)/shard_map/ppermute | solution.py:19
  175.5 21.0 %copy-start.11 = (s32[6]{0:T(128)S(1)}, s32[6]{0:T(128)}, u32[]{:S(2)}) copy-start(s32[6]{0:T(128)} %param.22) | copy-start | bytes 76
  183.2 10.6 %copy-start.12 = (pred[128]{0:T(512)(128)(4,1)S(1)}, pred[128]{0:T(512)(128)(4,1)}, u32[]{:S(2)}) copy-start(pred[128]{0:T(512)(128)(4,1)} %and.135) | copy-start | bytes 388
  240.7 12.7 %copy-start.1 = (s32[4,12,8,16]{3,2,1,0:T(8,128)S(1)}, s32[4,12,8,16]{3,2,1,0:T(8,128)}, u32[]{:S(2)}) copy-start(s32[4,12,8,16]{3,2,1,0:T(8,128)} %broadcast_maximum_fusion) | copy-start | bytes 73732
  282.9 36.7 %collective-permute-start.4 = (f32[1,3,2,12,12]{3,2,1,4,0:T(2,128)}, f32[1,3,2,12,12]{3,2,1,4,0:T(2,128)}, u32[]{:S(2)}, u32[]{:S(2)}) collective-permute-start(f32[1,3,2,12,12]{3,2,1,4,0:T(2,128)} %get-tuple-element.652), channel_id=1, source_target_pairs={{0,4},{4,8},{8,12},{12,16},{16,20},{20,24},{24,28},{1,5},{5,9},{9,... | collective-permute-start | bytes 10376 | tf_op jit(solution)/shard_map/ppermute | solution.py:16
  285.1 34.5 %collective-permute-start.5 = (f32[1,3,2,12,12]{3,2,1,4,0:T(2,128)}, f32[1,3,2,12,12]{3,2,1,4,0:T(2,128)}, u32[]{:S(2)}, u32[]{:S(2)}) collective-permute-start(f32[1,3,2,12,12]{3,2,1,4,0:T(2,128)} %get-tuple-element.653), channel_id=1, source_target_pairs={{4,0},{8,4},{12,8},{16,12},{20,16},{24,20},{28,24},{5,1},{9,5},{13... | collective-permute-start | bytes 10376 | tf_op jit(solution)/shard_map/ppermute | solution.py:19
  294.2 0.9 copy-start.4
  295.5 5.1 copy-start.10
  319.7 6.6 %copy-start.9 = (bf16[144,6,128]{2,0,1:T(8,128)(2,1)S(1)}, bf16[144,6,128]{2,0,1:T(8,128)(2,1)}, u32[]{:S(2)}) copy-start(bf16[144,6,128]{2,0,1:T(8,128)(2,1)} %get-tuple-element.649) | copy-start | bytes 663556
  320.7 6.7 %collective-permute-start.6 = (f32[1,3,8,2,12]{3,2,1,4,0:T(8,128)S(1)}, f32[1,3,8,2,12]{3,2,1,4,0:T(8,128)S(1)}, u32[]{:S(2)}, u32[]{:S(2)}) collective-permute-start(f32[1,3,8,2,12]{3,2,1,4,0:T(8,128)S(1)} %get-tuple-element.650), channel_id=1, source_target_pairs={{0,1},{1,2},{2,3},{4,5},{5,6},{6,7},{8,9},{9,10},{10,11},{12,13},{... | collective-permute-start | bytes 6920 | tf_op jit(solution)/shard_map/ppermute | solution.py:16
  322.7 7.5 %collective-permute-start.7 = (f32[1,3,8,2,12]{3,2,1,4,0:T(8,128)S(1)}, f32[1,3,8,2,12]{3,2,1,4,0:T(8,128)S(1)}, u32[]{:S(2)}, u32[]{:S(2)}) collective-permute-start(f32[1,3,8,2,12]{3,2,1,4,0:T(8,128)S(1)} %get-tuple-element.651), channel_id=1, source_target_pairs={{1,0},{2,1},{3,2},{5,4},{6,5},{7,6},{9,8},{10,9},{11,10},{13,12},{... | collective-permute-start | bytes 6920 | tf_op jit(solution)/shard_map/ppermute | solution.py:19
  515.4 2.0 copy-start.2
  526.6 2.2 copy-start.3
  530.8 2.0 copy-start.2
  542.0 2.2 copy-start.3
  546.1 2.0 copy-start.2
  557.4 2.2 copy-start.3
  561.5 2.0 copy-start.2
  572.7 2.2 copy-start.3
  576.9 2.0 copy-start.2
  588.1 2.2 copy-start.3
  592.2 2.0 copy-start.2
  603.5 2.2 copy-start.3
  607.6 2.0 copy-start.2
  618.8 2.2 copy-start.3
  623.0 2.0 copy-start.2
  634.2 2.2 copy-start.3
Sparse Core Ops, SparseCore 0:
  10.0 84.7 all-gather.1
where the time goes:
time: 656 us; the launch traced here: 647 us
  blocking collectives  180 us (27%)
  waiting for transfers between devices  152 us (23%)
  local copies, waits for them, and re-layouts  147 us (22%)
  matrix products  55.1 us (8%)
  other arithmetic  39.6 us (6%)
  loops' own time  36.7 us (6%)
  starting transfers between devices  21.4 us (3%)
  between operations  14.9 us (2%)
    all_gather x1, blocking collectives, shards(): stats_all = lax.all_gather(stat_wide, 'span', axis=0, tiled=True)  180 us
    all_gather x1, waiting for transfers between devices, shards(): everything = lax.all_gather(bundle, 'span', axis=0, tiled=True)  84.9 us
    ppermute x4, waiting for transfers between devices, padded(): lax.ppermute(lax.slice_in_dim(block, block.shape[dim] - width, None, axis...  55.6 us
    another operation x3, loops' own time, over_tiles(): result, _ = lax.scan(inner, carried, (piece, block_ids))  30.3 us
    unnamed x36, local copies, waits for them, and re-layouts  26.6 us
    dot_general x8, matrix products, key_run(): jnp.einsum('hqk,qhd->khd', slope, asking, preferred_element_type=jnp.floa...  20.5 us
    squeeze x10, local copies, waits for them, and re-layouts, over_tiles(): result, _ = lax.scan(inner, carried, (piece, block_ids))  19.7 us
    dynamic_slice x24, local copies, waits for them, and re-layouts, over_tiles(): result, _ = lax.scan(inner, carried, (piece, block_ids))  18.6 us
  transfers between devices with their start and end apart: 9, of which 6 were waited for; matrix products, arithmetic and copies ran while one was open for 9% of the time, Pallas kernels for 0%

commit v1 on v0

v1 whole, which is shorter than its diff:
```python
import functools
import math

import jax
import jax.numpy as jnp
import numpy as np
from jax import lax
from jax.experimental import pallas as pl
from jax.experimental.pallas import tpu as pltpu
from jax.sharding import PartitionSpec as P

MESH = pl.DeviceIdType.MESH
BF = jnp.bfloat16
F32 = jnp.float32

NB = 8
NA = 8
NW = 4
FR = 3
TH = 4
TW = 12
OWN = TH * TW
WIDE = 128
DH = 128
HEADS = 6
HIDE = -1e30
SCALE = 1.0 / math.sqrt(DH)
LOG2E = math.log2(math.e)
OFFSETS = (4, 3, -3, 2, -2, 1, -1, 0)


def positions():
    order = list(range(TW)) + [-2, -1, TW, TW + 1]
    rows, cols = [], []
    for column in order:
        for row in range(TH):
            rows.append(row)
            cols.append(column)
    for first in (-2, TH):
        for column in order:
            for step in range(2):
                rows.append(first + step)
                cols.append(column)
    return np.array(rows, np.int32), np.array(cols, np.int32)


def place():
    return lax.axis_index("span"), lax.axis_index("ha"), lax.axis_index("wa")


def busy(z):
    return lax.rem(z, 4) != 3


def head_at(z):
    return z - z // 4


def at_head(h):
    return h + h // 3


def shift_up(i, n):
    return lax.rem(i + 1, n)


def shift_down(i, n):
    return lax.rem(i + n - 1, n)


def greet(z, a, w):
    barrier = pltpu.get_barrier_semaphore()
    for step in range(1, NB):
        pl.semaphore_signal(
            barrier, inc=1, device_id=(lax.rem(z + step, NB), a, w), device_id_type=MESH
        )
    for other in (shift_up(a, NA), shift_down(a, NA)):
        pl.semaphore_signal(barrier, inc=1, device_id=(z, other, w), device_id_type=MESH)
    for other in (shift_up(w, NW), shift_down(w, NW)):
        pl.semaphore_signal(barrier, inc=1, device_id=(z, a, other), device_id_type=MESH)
    pl.semaphore_wait(barrier, NB - 1 + 4)


def picker(shape, edge_dim):
    e = lax.broadcasted_iota(jnp.int32, shape, edge_dim)
    p = lax.broadcasted_iota(jnp.int32, shape, 1 - edge_dim)
    low = e & 31
    wanted = (low >> 1) * 4 + (e >> 5) * 2 + (low & 1)
    return (p == wanted).astype(F32).astype(BF)


def head_columns(h):
    return pl.ds(pl.multiple_of(h * DH, DH), DH)


def remote(src, dst, send, recv, to):
    return pltpu.make_async_remote_copy(
        src_ref=src, dst_ref=dst, send_sem=send, recv_sem=recv, device_id=to, device_id_type=MESH
    )


def gather_kernel(
    k_in, v_in, q_in, g_in, kv, qg, edge, z_send, z_recv, c_send, c_recv, r_send, r_recv
):
    z, a, w = place()
    arrays = (k_in, v_in, q_in, g_in)
    greet(z, a, w)
    pick = picker((64, 64), 0)

    def target(i, c):
        if i < 2:
            return kv.at[i, c, :, 0:OWN]
        return qg.at[i - 2, c]

    def z_copy(i, slot, t):
        return remote(
            arrays[i].at[:, :, head_columns(head_at(t))],
            target(i, z),
            z_send.at[i, slot],
            z_recv.at[i, z],
            (t, a, w),
        )

    def z_local(i):
        return pltpu.make_async_copy(
            arrays[i].at[:, :, head_columns(head_at(z))], target(i, z), z_recv.at[i, z]
        )

    def z_arrive(i, c):
        remote(target(i, c), target(i, c), z_send.at[i, 0], z_recv.at[i, c], (z, a, w)).wait_recv()

    def col_copy(side, c):
        if side == 0:
            src, dst, to = kv.at[:, c, :, 0:8], kv.at[:, c, :, 56:64], shift_down(w, NW)
        else:
            src, dst, to = kv.at[:, c, :, 40:48], kv.at[:, c, :, 48:56], shift_up(w, NW)
        return remote(src, dst, c_send.at[side, c], c_recv.at[side, c], (z, a, to))

    def row_copy(side, c):
        if side == 0:
            dst, to = kv.at[:, c, :, 96:128], shift_down(a, NA)
        else:
            dst, to = kv.at[:, c, :, 64:96], shift_up(a, NA)
        return remote(
            edge.at[side, :, c], dst, r_send.at[side, c], r_recv.at[side, c], (z, to, w)
        )

    for pair in ((0, 1), (2, 3)):
        for slot, offset in enumerate(OFFSETS):
            t = lax.rem(z + offset + NB, NB)

            @pl.when(busy(t))
            def _():
                for i in pair:
                    if offset == 0:
                        z_local(i).start()
                    else:
                        z_copy(i, slot, t).start()

    @pl.when(busy(z))
    def _():
        def cols_out(c, own):
            for i in range(2):
                if own:
                    z_local(i).wait()
                else:
                    z_arrive(i, c)
            for side in range(2):
                col_copy(side, c).start()

        def rows_out(c):
            for side in range(2):
                col_copy(side, c).wait_recv()
            for i in range(2):
                for f in range(FR):
                    out = jnp.dot(pick, kv[i, c, f, 0:64, :], preferred_element_type=F32)
                    out = out.astype(BF)
                    edge[0, i, c, f] = out[0:32]
                    edge[1, i, c, f] = out[32:64]
            for side in range(2):
                row_copy(side, c).start()

        order = (0,) + OFFSETS[:-1]
        blocks = [lax.rem(z + offset + NB, NB) for offset in order]
        for n, c in enumerate(blocks):
            cols_out(c, n == 0)
            if n > 0:
                rows_out(blocks[n - 1])
        rows_out(blocks[-1])
        for n, c in enumerate(blocks):
            for side in range(2):
                row_copy(side, c).wait_recv()
            for i in (2, 3):
                if n == 0:
                    z_local(i).wait()
                else:
                    z_arrive(i, c)
        for n, c in enumerate(blocks):
            for side in range(2):
                col_copy(side, c).wait_send()
                row_copy(side, c).wait_send()

    for slot, offset in enumerate(OFFSETS[:-1]):
        t = lax.rem(z + offset + NB, NB)

        @pl.when(busy(t))
        def _():
            for i in range(4):
                z_copy(i, slot, t).wait_send()


def nt(x, y):
    return lax.dot_general(x, y, (((1,), (1,)), ((), ())), preferred_element_type=F32)


def tn(x, y):
    return lax.dot_general(x, y, (((0,), (0,)), ((), ())), preferred_element_type=F32)


def attend_kernel(
    kv,
    qg,
    near,
    dead,
    att_out,
    dq_out,
    dk_out,
    dv_out,
    scores,
    acc,
    ad_stage,
    row_stage,
    row_in,
    col_stage,
    col_in,
    fin_stage,
    ad_send,
    ad_recv,
    fin_send,
    fin_recv,
    r_send,
    r_recv,
    c_send,
    c_recv,
):
    z, a, w = place()
    queries = FR * OWN
    keys = FR * WIDE
    ad_outs = (att_out, dq_out)
    fin_outs = (dk_out, dv_out)
    greet(z, a, w)
    spread = picker((64, 64), 1)
    me = head_at(z)

    def out_copy(outs, stage, send, recv, i, c):
        return remote(
            stage.at[i, c],
            outs[i].at[:, :, head_columns(me)],
            send.at[i, c],
            recv.at[i, me],
            (c, a, w),
        )

    def out_local(outs, stage, recv, i):
        return pltpu.make_async_copy(
            stage.at[i, z], outs[i].at[:, :, head_columns(me)], recv.at[i, me]
        )

    def out_start(outs, stage, send, recv, c):
        @pl.when(c == z)
        def _():
            for i in range(2):
                out_local(outs, stage, recv, i).start()

        @pl.when(c != z)
        def _():
            for i in range(2):
                out_copy(outs, stage, send, recv, i, c).start()

    def row_copy(side, c):
        to = shift_down(a, NA) if side == 0 else shift_up(a, NA)
        return remote(
            row_stage.at[side, :, c],
            row_in.at[side, :, c],
            r_send.at[side, c],
            r_recv.at[side, c],
            (z, to, w),
        )

    def col_copy(side, c):
        to = shift_down(w, NW) if side == 0 else shift_up(w, NW)
        return remote(
            col_stage.at[side, :, c],
            col_in.at[side, :, c],
            c_send.at[side, c],
            c_recv.at[side, c],
            (z, a, to),
        )

    def compute(c):
        query = qg[0, c].reshape(queries, DH)
        upstream = qg[1, c].reshape(queries, DH)
        near_rows = jnp.concatenate([near[...]] * FR, axis=0)

        def score_step(j, top):
            s = nt(query, kv[0, j].reshape(keys, DH))
            for f in range(FR):
                part = s[:, f * WIDE : (f + 1) * WIDE] + (near_rows + dead[pl.ds(j * FR + f, 1), :])
                scores[j, :, f * WIDE : (f + 1) * WIDE] = part
                top = jnp.maximum(top, part)
            return top

        top = lax.fori_loop(0, c + 1, score_step, jnp.full((queries, WIDE), HIDE, F32))
        top = jnp.max(top, axis=1, keepdims=True)

        def weight_step(j, carried):
            total, out = carried
            weight = jnp.exp2((scores[j] - top) * (SCALE * LOG2E))
            scores[j] = weight
            for f in range(FR):
                total = total + weight[:, f * WIDE : (f + 1) * WIDE]
            out = out + jnp.dot(
                weight.astype(BF), kv[1, j].reshape(keys, DH), preferred_element_type=F32
            )
            return total, out

        zero = jnp.zeros((queries, WIDE), F32)
        total, out = lax.fori_loop(0, c + 1, weight_step, (zero, zero))
        total = jnp.sum(total, axis=1, keepdims=True)
        attended = (out / total).astype(BF)
        delta = jnp.sum(upstream.astype(F32) * attended.astype(F32), axis=1, keepdims=True)
        ad_stage[0, c] = attended.reshape(FR, OWN, DH)
        inverse = 1.0 / total

        def grad_step(j, grad_q):
            prob = scores[j] * inverse
            push = nt(upstream, kv[1, j].reshape(keys, DH))
            slope = (prob * (push - delta)).astype(BF)
            acc[1, j] += tn(prob.astype(BF), upstream).reshape(FR, WIDE, DH)
            acc[0, j] += tn(slope, query).reshape(FR, WIDE, DH)
            return grad_q + jnp.dot(
                slope, kv[0, j].reshape(keys, DH), preferred_element_type=F32
            )

        grad_q = lax.fori_loop(0, c + 1, grad_step, zero)
        ad_stage[1, c] = (grad_q * SCALE).astype(BF).reshape(FR, OWN, DH)

    def rows_out(c):
        for i in range(2):
            for f in range(FR):
                row_stage[0, i, c, f] = acc[i, c, f, 64:96, :].astype(BF)
                row_stage[1, i, c, f] = acc[i, c, f, 96:128, :].astype(BF)
        for side in range(2):
            row_copy(side, c).start()

    def cols_out(c):
        for side in range(2):
            row_copy(side, c).wait_recv()
        for i in range(2):
            for f in range(FR):
                edge = jnp.concatenate([row_in[1, i, c, f], row_in[0, i, c, f]], axis=0)
                acc[i, c, f, 0:64, :] += jnp.dot(spread, edge, preferred_element_type=F32)
                col_stage[0, i, c, f] = acc[i, c, f, 48:56, :].astype(BF)
                col_stage[1, i, c, f] = acc[i, c, f, 56:64, :].astype(BF)
        for side in range(2):
            col_copy(side, c).start()

    def finish(c):
        for side in range(2):
            col_copy(side, c).wait_recv()
        for i in range(2):
            factor = SCALE if i == 0 else 1.0
            for f in range(FR):
                whole = acc[i, c, f, 0:OWN, :]
                left = whole[0:8] + col_in[1, i, c, f].astype(F32)
                right = whole[40:48] + col_in[0, i, c, f].astype(F32)
                whole = jnp.concatenate([left, whole[8:40], right], axis=0)
                fin_stage[i, c, f] = (whole * factor).astype(BF)
        out_start(fin_outs, fin_stage, fin_send, fin_recv, c)

    @pl.when(busy(z))
    def _():
        acc[...] = jnp.zeros_like(acc)

        def step(n, _):
            c = NB - 1 - n
            compute(c)
            out_start(ad_outs, ad_stage, ad_send, ad_recv, c)
            rows_out(c)

            @pl.when(n >= 1)
            def _():
                cols_out(c + 1)

            @pl.when(n >= 2)
            def _():
                finish(c + 2)

            return 0

        lax.fori_loop(0, NB, step, 0)
        cols_out(0)
        finish(1)
        finish(0)

        def drain(c, _):
            for side in range(2):
                row_copy(side, c).wait_send()
                col_copy(side, c).wait_send()

            @pl.when(c != z)
            def _():
                for i in range(2):
                    out_copy(ad_outs, ad_stage, ad_send, ad_recv, i, c).wait_send()
                    out_copy(fin_outs, fin_stage, fin_send, fin_recv, i, c).wait_send()

            return 0

        lax.fori_loop(0, NB, drain, 0)

    for h in range(HEADS):
        for outs, stage, send, recv in (
            (ad_outs, ad_stage, ad_send, ad_recv),
            (fin_outs, fin_stage, fin_send, fin_recv),
        ):
            for i in range(2):
                view = outs[i].at[:, :, h * DH : (h + 1) * DH]
                pltpu.make_async_copy(view, view, recv.at[i, h]).wait()


def packed(array):
    frames, tile_h, tile_w, width = array.shape[1:]
    return jnp.transpose(array[0], (0, 2, 1, 3)).reshape(frames, tile_h * tile_w, width)


def unpacked(array):
    frames, rows, width = array.shape
    return jnp.transpose(array.reshape(frames, TW, TH, width), (0, 2, 1, 3))[None]


def shards(queries, cache_keys, cache_values, grad_attended, radius, frame_count):
    z, a, w = place()
    rows, cols = positions()
    own_radius = radius[jnp.minimum(head_at(z), HEADS - 1)]
    reach = np.maximum(
        np.abs(rows[:OWN, None] - rows[None, :]), np.abs(cols[:OWN, None] - cols[None, :])
    )
    full_rows, full_cols = rows[None, :] + a * TH, cols[None, :] + w * TW
    inside = (full_rows >= 0) & (full_rows < TH * NA) & (full_cols >= 0) & (full_cols < TW * NW)
    near = jnp.where((reach <= own_radius) & inside, 0.0, HIDE).astype(F32)
    live = jnp.arange(FR)[None, :] < frame_count[:, None]
    dead = jnp.where(live.reshape(NB * FR, 1), 0.0, HIDE).astype(F32)
    dead = jnp.broadcast_to(dead, (NB * FR, WIDE))

    vmem = pl.BlockSpec(memory_space=pltpu.VMEM)
    anywhere = pl.BlockSpec(memory_space=pl.ANY)
    dma = pltpu.SemaphoreType.DMA
    kv, qg = pl.pallas_call(
        gather_kernel,
        out_shape=(
            jax.ShapeDtypeStruct((2, NB, FR, WIDE, DH), BF),
            jax.ShapeDtypeStruct((2, NB, FR, OWN, DH), BF),
        ),
        in_specs=[anywhere] * 4,
        out_specs=(vmem, vmem),
        scratch_shapes=[
            pltpu.VMEM((2, 2, NB, FR, 32, DH), BF),
            dma((4, NB)),
            dma((4, NB)),
            dma((2, NB)),
            dma((2, NB)),
            dma((2, NB)),
            dma((2, NB)),
        ],
        compiler_params=pltpu.CompilerParams(collective_id=0, has_side_effects=True),
        name="gather",
    )(packed(cache_keys), packed(cache_values), packed(queries), packed(grad_attended))

    flat = jax.ShapeDtypeStruct((FR, OWN, HEADS * DH), BF)
    outs = pl.pallas_call(
        attend_kernel,
        out_shape=(flat,) * 4,
        in_specs=[vmem] * 4,
        out_specs=(anywhere,) * 4,
        scratch_shapes=[
            pltpu.VMEM((NB, FR * OWN, FR * WIDE), F32),
            pltpu.VMEM((2, NB, FR, WIDE, DH), F32),
            pltpu.VMEM((2, NB, FR, OWN, DH), BF),
            pltpu.VMEM((2, 2, NB, FR, 32, DH), BF),
            pltpu.VMEM((2, 2, NB, FR, 32, DH), BF),
            pltpu.VMEM((2, 2, NB, FR, 8, DH), BF),
            pltpu.VMEM((2, 2, NB, FR, 8, DH), BF),
            pltpu.VMEM((2, NB, FR, OWN, DH), BF),
            dma((2, NB)),
            dma((2, NB)),
            dma((2, NB)),
            dma((2, NB)),
            dma((2, NB)),
            dma((2, NB)),
            dma((2, NB)),
            dma((2, NB)),
        ],
        compiler_params=pltpu.CompilerParams(collective_id=1, has_side_effects=True),
        name="attend",
    )(kv, qg, near, dead)
    attended, grad_queries, grad_keys, grad_values = (unpacked(x) for x in outs)
    return attended, grad_queries, grad_keys, grad_values


def solution(mesh):
    tiled = P("span", None, "ha", "wa", None)
    return jax.shard_map(
        shards,
        mesh=mesh,
        in_specs=(tiled,) * 4 + (P(), P()),
        out_specs=(tiled,) * 4,
        check_vma=False,
    )
```

time: 656 us -> 124 us (0.19)
  the two profiles are of different devices: /device:TPU:2 before, /device:TPU:1 now
where the time goes in v1:
time: 124 us; the launch traced here: 123 us
  Pallas kernels  104 us (84%)
  local copies, waits for them, and re-layouts  14.5 us (12%)
  other arithmetic  3.4 us (3%)
    pallas_call x1, Pallas kernels, shards(): pl.pallas_call(attend_kernel, out_shape=(flat,) * 4, in_specs=[vmem] * 4,...  60.9 us
    pallas_call x1, Pallas kernels, shards(): pl.pallas_call(gather_kernel, out_shape=(jax.ShapeDtypeStruct((2, NB, FR,...  43.5 us
    reshape x4, local copies, waits for them, and re-layouts, unpacked(): array.reshape(frames, TW, TH, width)  6.7 us
    reshape x4, local copies, waits for them, and re-layouts, packed(): jnp.transpose(array[0], (0, 2, 1, 3))  5.76 us

profile of v1, /device:TPU:1, one launch (start us, length us, event | category | flops | bytes accessed | tf_op | source)
XLA Modules:
  0.0 123.0 jit_solution(9962580858433249653)
XLA Ops:
  0.6 0.0 copy-start
  0.7 1.3 %dynamic_slice.3 = s32[1]{0:T(128)} dynamic-slice(s32[6]{0:T(128)} %param.13, s32[]{:T(128)S(6)} %select_n.25), dynamic_slice_sizes={1} | dynamic-slice | bytes 12 | tf_op jit(solution)/shard_map/dynamic_slice | solution.py:444
  2.0 0.7 and_bitcast_fusion
  2.6 0.7 fusion
  3.4 0.1 select_n.28
  3.4 0.7 broadcast_in_dim.39.dead
  4.1 2.0 %and_select_fusion.near = f32[48,128]{1,0:T(8,128)} fusion(s32[48,128]{1,0:T(8,128)} %constant.54.clone, s32[]{:T(128)} %bitcast.8, pred[128]{0:T(512)(128)(4,1)S(1)} %and_bitcast_fusion), kind=kLoop, calls=%fused_computation | loop fusion | flops 18432 | bytes 49284 | tf_op jit(solution)/shard_map/jit(_where)/select_n | solution.py:450
  6.1 1.7 %reshape.54.q_in = bf16[3,48,768]{2,1,0:T(8,128)(2,1)} reshape(bf16[3,12,4,768]{3,2,1,0:T(4,128)(2,1)} %bitcast.27) | data formatting | bytes 442368 | tf_op jit(solution)/shard_map/reshape | solution.py:433
  7.8 1.7 %reshape.52.k_in = bf16[3,48,768]{2,1,0:T(8,128)(2,1)} reshape(bf16[3,12,4,768]{3,2,1,0:T(4,128)(2,1)} %bitcast.28) | data formatting | bytes 442368 | tf_op jit(solution)/shard_map/reshape | solution.py:433
  9.5 1.7 %reshape.53.v_in = bf16[3,48,768]{2,1,0:T(8,128)(2,1)} reshape(bf16[3,12,4,768]{3,2,1,0:T(4,128)(2,1)} %bitcast.29) | data formatting | bytes 442368 | tf_op jit(solution)/shard_map/reshape | solution.py:433
  11.1 0.0 copy-done
  11.2 0.7 reshape.55.g_in
  11.9 43.5 %gather.1 = (bf16[2,8,3,128,128]{4,3,2,1,0:T(8,128)(2,1)}, bf16[2,8,3,48,128]{4,3,2,1,0:T(8,128)(2,1)}) custom-call(bf16[3,48,768]{2,1,0:T(8,128)(2,1)} %reshape.52.k_in, bf16[3,48,768]{2,1,0:T(8,128)(2,1)} %reshape.53.v_in, bf16[3,48,768]{2,1,0:T(8,128)(2,1)} %reshape.54.q_in, bf16[3,48,768]{2,1,0:T(8,128)(2,1)} %reshape.55.g_in), custom_call_target="tpu_custom_call" | custom-call | tf_op jit(solution)/shard_map/gather/pallas_call | solution.py:458
  55.4 60.9 %attend.1 = (bf16[3,48,768]{2,1,0:T(8,128)(2,1)}, bf16[3,48,768]{2,1,0:T(8,128)(2,1)}, bf16[3,48,768]{2,1,0:T(8,128)(2,1)}, bf16[3,48,768]{2,1,0:T(8,128)(2,1)}) custom-call(bf16[2,8,3,128,128]{4,3,2,1,0:T(8,128)(2,1)} %get-tuple-element.10.kv, bf16[2,8,3,48,128]{4,3,2,1,0:T(8,128)(2,1)} %get-tuple-element.11.qg, f32[48,128]{1,0:T(8,128)} %and_select_fusion.near, ...), custom_call_target="tpu_custom_call" | custom-call | tf_op jit(solution)/shard_map/attend/pallas_call | solution.py:480
  116.3 1.7 %reshape.56 = bf16[3,12,4,768]{3,2,1,0:T(4,128)(2,1)} reshape(bf16[3,48,768]{2,1,0:T(8,128)(2,1)} %get-tuple-element.12) | data formatting | bytes 442368 | tf_op jit(solution)/shard_map/reshape | solution.py:438
  118.0 1.7 %reshape.57 = bf16[3,12,4,768]{3,2,1,0:T(4,128)(2,1)} reshape(bf16[3,48,768]{2,1,0:T(8,128)(2,1)} %get-tuple-element.13) | data formatting | bytes 442368 | tf_op jit(solution)/shard_map/reshape | solution.py:438
  119.7 1.7 %reshape.58 = bf16[3,12,4,768]{3,2,1,0:T(4,128)(2,1)} reshape(bf16[3,48,768]{2,1,0:T(8,128)(2,1)} %get-tuple-element.14) | data formatting | bytes 442368 | tf_op jit(solution)/shard_map/reshape | solution.py:438
  121.4 1.7 %reshape.59 = bf16[3,12,4,768]{3,2,1,0:T(4,128)(2,1)} reshape(bf16[3,48,768]{2,1,0:T(8,128)(2,1)} %get-tuple-element.15) | data formatting | bytes 442368 | tf_op jit(solution)/shard_map/reshape | solution.py:438
Async XLA Ops:
  0.6 10.5 %copy-start = (bf16[1,3,4,12,768]{4,2,3,1,0:T(4,128)(2,1)S(1)}, bf16[1,3,4,12,768]{4,2,3,1,0:T(4,128)(2,1)}, u32[]{:S(2)}) copy-start(bf16[1,3,4,12,768]{4,2,3,1,0:T(4,128)(2,1)} %param.12) | copy-start | bytes 663556

commit v2 on v1

v2 whole, which is shorter than its diff:
```python
import math

import jax
import jax.numpy as jnp
from jax import lax
from jax.experimental import pallas as pl
from jax.experimental.pallas import tpu as pltpu
from jax.sharding import PartitionSpec as P

MESH = pl.DeviceIdType.MESH
BF = jnp.bfloat16
F32 = jnp.float32

NB = 8
NA = 8
NW = 4
FR = 3
TH = 4
TW = 12
OWN = TH * TW
WIDE = 128
DH = 128
HEADS = 6
BLOCK = FR * OWN
KEYS = FR * WIDE
GROUP = 128
HIDE = -1e30
SCALE = 1.0 / math.sqrt(DH)
LOG2E = math.log2(math.e)
OFFSETS = (4, 3, -3, 2, -2, 1, -1, 0)


def place():
    return lax.axis_index("span"), lax.axis_index("ha"), lax.axis_index("wa")


def busy(z):
    return lax.rem(z, 4) != 3


def head_at(z):
    return z - z // 4


def at_head(h):
    return h + h // 3


def shift_up(i, n):
    return lax.rem(i + 1, n)


def shift_down(i, n):
    return lax.rem(i + n - 1, n)


def greet(z, a, w):
    barrier = pltpu.get_barrier_semaphore()
    for step in range(1, NB):
        pl.semaphore_signal(
            barrier, inc=1, device_id=(lax.rem(z + step, NB), a, w), device_id_type=MESH
        )
    for other in (shift_up(a, NA), shift_down(a, NA)):
        pl.semaphore_signal(barrier, inc=1, device_id=(z, other, w), device_id_type=MESH)
    for other in (shift_up(w, NW), shift_down(w, NW)):
        pl.semaphore_signal(barrier, inc=1, device_id=(z, a, other), device_id_type=MESH)
    pl.semaphore_wait(barrier, NB - 1 + 4)


def picker(shape, edge_dim):
    e = lax.broadcasted_iota(jnp.int32, shape, edge_dim)
    p = lax.broadcasted_iota(jnp.int32, shape, 1 - edge_dim)
    low = e & 31
    wanted = (low >> 1) * 4 + (e >> 5) * 2 + (low & 1)
    return (p == wanted).astype(F32).astype(BF)


def head_columns(h):
    return pl.ds(pl.multiple_of(h * DH, DH), DH)


def remote(src, dst, send, recv, to):
    return pltpu.make_async_remote_copy(
        src_ref=src, dst_ref=dst, send_sem=send, recv_sem=recv, device_id=to, device_id_type=MESH
    )


def nt(x, y):
    return lax.dot_general(x, y, (((1,), (1,)), ((), ())), preferred_element_type=F32)


def mm(x, y):
    return jnp.dot(x, y, preferred_element_type=F32)


def arrived(view, sem):
    pltpu.make_async_copy(view, view, sem).wait()


def reach_table(near, radius, a, w):
    p = lax.broadcasted_iota(jnp.int32, (WIDE, GROUP), 0)
    lane = lax.broadcasted_iota(jnp.int32, (WIDE, GROUP), 1)
    edge = p >= 64
    low = p & 31
    column = jnp.where(edge, low >> 1, p >> 2)
    row = jnp.where(edge, (low & 1) + jnp.where(p >= 96, TH, -2), p & 3)
    column = column - jnp.where(column >= 14, 2, jnp.where(column >= 12, 14, 0))
    full_row, full_column = row + a * TH, column + w * TW
    inside = (full_row >= 0) & (full_row < TH * NA) & (full_column >= 0)
    inside = inside & (full_column < TW * NW)
    for g in range(3):
        spot = lane + (g * GROUP) % OWN
        for _ in range(3):
            spot = jnp.where(spot >= OWN, spot - OWN, spot)
        gap = jnp.maximum(jnp.abs(row - (spot & 3)), jnp.abs(column - (spot >> 2)))
        near[g] = jnp.where((gap <= radius) & inside, 0.0, HIDE).astype(F32)


def fused_kernel(
    radius,
    count,
    k_in,
    v_in,
    q_in,
    g_in,
    att_out,
    dq_out,
    dk_out,
    dv_out,
    kv,
    kvt,
    qg,
    near,
    pair,
    scores,
    pushes,
    acc,
    edge,
    ad_stage,
    row_stage,
    row_in,
    col_stage,
    col_in,
    fin_stage,
    z_send,
    z_recv,
    c_send,
    c_recv,
    r_send,
    r_recv,
    ad_send,
    ad_recv,
    fin_send,
    fin_recv,
    gr_send,
    gr_recv,
    gc_send,
    gc_recv,
):
    z, a, w = place()
    me = head_at(z)
    arrays = (k_in, v_in, q_in, g_in)
    ad_outs = (att_out, dq_out)
    fin_outs = (dk_out, dv_out)
    greet(z, a, w)

    def block_rows(c):
        return pl.ds(pl.multiple_of(c * BLOCK, 16), BLOCK)

    def target(i, c):
        if i < 2:
            return kv.at[i, c, :, 0:OWN]
        return qg.at[i - 2, block_rows(c)]

    def source(i, t):
        if i < 2:
            return arrays[i].at[:, :, head_columns(head_at(t))]
        return arrays[i].at[:, head_columns(head_at(t))]

    def z_copy(i, slot, t):
        return remote(source(i, t), target(i, z), z_send.at[i, slot], z_recv.at[i, z], (t, a, w))

    def z_local(i):
        return pltpu.make_async_copy(source(i, z), target(i, z), z_recv.at[i, z])

    def col_copy(side, c):
        if side == 0:
            src, dst, to = kv.at[:, c, :, 0:8], kv.at[:, c, :, 56:64], shift_down(w, NW)
        else:
            src, dst, to = kv.at[:, c, :, 40:48], kv.at[:, c, :, 48:56], shift_up(w, NW)
        return remote(src, dst, c_send.at[side, c], c_recv.at[side, c], (z, a, to))

    def row_copy(side, c):
        if side == 0:
            dst, to = kv.at[:, c, :, 96:128], shift_down(a, NA)
        else:
            dst, to = kv.at[:, c, :, 64:96], shift_up(a, NA)
        return remote(
            edge.at[side, :, c], dst, r_send.at[side, c], r_recv.at[side, c], (z, to, w)
        )

    for kinds in ((0, 1), (2, 3)):
        for slot, offset in enumerate(OFFSETS):
            t = lax.rem(z + offset + NB, NB)

            @pl.when(busy(t))
            def _():
                for i in kinds:
                    if offset == 0:
                        z_local(i).start()
                    else:
                        z_copy(i, slot, t).start()

    def gather():
        pick = picker((64, 64), 0)

        def cols_first(c):
            for i in range(2):
                arrived(target(i, c), z_recv.at[i, c])
            for side in range(2):
                col_copy(side, c).start()

        def rows_next(c):
            for side in range(2):
                col_copy(side, c).wait_recv()
            for i in range(2):
                for f in range(FR):
                    out = mm(pick, kv[i, c, f, 0:64, :]).astype(BF)
                    edge[0, i, c, f] = out[0:32]
                    edge[1, i, c, f] = out[32:64]
            for side in range(2):
                row_copy(side, c).start()

        def turn(c):
            for side in range(2):
                row_copy(side, c).wait_recv()
            for i in range(2):
                for f in range(FR):
                    kvt[i, c, :, f * WIDE : (f + 1) * WIDE] = kv[i, c, f].T

        order = (0,) + OFFSETS[:-1]
        blocks = [lax.rem(z + offset + NB, NB) for offset in order]
        for n in range(NB + 2):
            if n < NB:
                cols_first(blocks[n])
            if 1 <= n <= NB:
                rows_next(blocks[n - 1])
            if n >= 2:
                turn(blocks[n - 2])

    def out_copy(outs, view, send, recv, i, c):
        return remote(
            view(i, c), outs[i].at[:, head_columns(me)], send.at[i, c], recv.at[i, me], (c, a, w)
        )

    def out_start(outs, view, send, recv, c):
        @pl.when(c == z)
        def _():
            for i in range(2):
                pltpu.make_async_copy(
                    view(i, c), outs[i].at[:, head_columns(me)], recv.at[i, me]
                ).start()

        @pl.when(c != z)
        def _():
            for i in range(2):
                out_copy(outs, view, send, recv, i, c).start()

    def ad_view(i, c):
        return ad_stage.at[i, block_rows(c)]

    def fin_view(i, c):
        return fin_stage.at[i, c]

    ad = (ad_outs, ad_view, ad_send, ad_recv)
    fin = (fin_outs, fin_view, fin_send, fin_recv)

    def back_rows(side, c):
        to = shift_down(a, NA) if side == 0 else shift_up(a, NA)
        return remote(
            row_stage.at[side, :, c],
            row_in.at[side, :, c],
            gr_send.at[side, c],
            gr_recv.at[side, c],
            (z, to, w),
        )

    def back_cols(side, c):
        to = shift_down(w, NW) if side == 0 else shift_up(w, NW)
        return remote(
            col_stage.at[side, :, c],
            col_in.at[side, :, c],
            gc_send.at[side, c],
            gc_recv.at[side, c],
            (z, a, to),
        )

    def compute(g):
        rows = pl.ds(pl.multiple_of(g * GROUP, GROUP), GROUP)
        upstream = qg[1, rows, :]
        pair[0:GROUP, 0:DH] = qg[0, rows, :]
        pair[GROUP : 2 * GROUP, DH : 2 * DH] = upstream
        chunks = jnp.minimum(g, NB - 1) + 1
        lane = lax.broadcasted_iota(jnp.int32, (1, GROUP), 1)
        pattern = lax.rem(g, 3)

        def both(j):
            return jnp.concatenate(
                [kv[0, j].reshape(KEYS, DH), kv[1, j].reshape(KEYS, DH)], axis=1
            )

        def folded(x, op):
            return op(x.reshape(x.shape[0] // 8, 8, GROUP), axis=0)

        def score_step(j, top):
            r = nt(both(j), pair[...])
            causal = jnp.where(lane + (g * GROUP - j * BLOCK) >= 0, 0.0, HIDE).astype(F32)
            live = count[j]
            for f in range(FR):
                hidden = causal + jnp.where(f < live, 0.0, HIDE).astype(F32)
                part = slice(f * WIDE, (f + 1) * WIDE)
                s = r[part, 0:GROUP] + (near[pattern] + hidden)
                scores[j, part, :] = s
                top = jnp.maximum(top, folded(s, jnp.max))
            pushes[j] = r[:, GROUP:]
            return top

        top = lax.fori_loop(0, chunks, score_step, jnp.full((8, GROUP), HIDE, F32))
        top = jnp.max(top, axis=0, keepdims=True)

        def weight_step(j, carried):
            total, out = carried
            weight = jnp.exp2((scores[j] - top) * (SCALE * LOG2E))
            scores[j] = weight
            return total + folded(weight, jnp.sum), out + mm(kvt[1, j], weight.astype(BF))

        zero = jnp.zeros((DH, GROUP), F32)
        total, out = lax.fori_loop(
            0, chunks, weight_step, (jnp.zeros((8, GROUP), F32), zero)
        )
        total = jnp.sum(total, axis=0, keepdims=True)
        attended = (out / total).astype(BF)
        delta = jnp.sum(
            upstream.T.astype(F32) * attended.astype(F32), axis=0, keepdims=True
        )
        ad_stage[0, rows, :] = attended.T
        inverse = 1.0 / total

        def grad_step(j, grad_q):
            prob = scores[j] * inverse
            slope = (prob * (pushes[j] - delta)).astype(BF)
            acc[j] += mm(jnp.concatenate([slope, prob.astype(BF)], axis=1), pair[...])
            return grad_q + mm(kvt[0, j], slope)

        grad_q = lax.fori_loop(0, chunks, grad_step, zero)
        ad_stage[1, rows, :] = (grad_q * SCALE).astype(BF).T

    def part_of(i):
        return slice(i * DH, (i + 1) * DH)

    def rows_out(c):
        for i in range(2):
            for f in range(FR):
                at = f * WIDE
                row_stage[0, i, c, f] = acc[c, at + 64 : at + 96, part_of(i)].astype(BF)
                row_stage[1, i, c, f] = acc[c, at + 96 : at + 128, part_of(i)].astype(BF)
        for side in range(2):
            back_rows(side, c).start()

    def cols_out(c):
        spread = picker((64, 64), 1)
        for side in range(2):
            back_rows(side, c).wait_recv()
        for i in range(2):
            for f in range(FR):
                at = f * WIDE
                border = jnp.concatenate([row_in[1, i, c, f], row_in[0, i, c, f]], axis=0)
                acc[c, at : at + 64, part_of(i)] += mm(spread, border)
                col_stage[0, i, c, f] = acc[c, at + 48 : at + 56, part_of(i)].astype(BF)
                col_stage[1, i, c, f] = acc[c, at + 56 : at + 64, part_of(i)].astype(BF)
        for side in range(2):
            back_cols(side, c).start()

    def finish(c):
        for side in range(2):
            back_cols(side, c).wait_recv()
        for i in range(2):
            factor = SCALE if i == 0 else 1.0
            for f in range(FR):
                whole = acc[c, f * WIDE : f * WIDE + OWN, part_of(i)]
                left = whole[0:8] + col_in[1, i, c, f].astype(F32)
                right = whole[40:48] + col_in[0, i, c, f].astype(F32)
                whole = jnp.concatenate([left, whole[8:40], right], axis=0)
                fin_stage[i, c, f * OWN : (f + 1) * OWN, :] = (whole * factor).astype(BF)
        out_start(*fin, c)

    @pl.when(busy(z))
    def _():
        reach_table(near, radius[me], a, w)
        pair[...] = jnp.zeros_like(pair)
        acc[...] = jnp.zeros_like(acc)
        gather()

        def step(n, _):
            g = NB - n

            @pl.when(g >= 1)
            def _():
                for i in (2, 3):
                    arrived(target(i, g - 1), z_recv.at[i, g - 1])

            compute(g)

            @pl.when(g <= NB - 1)
            def _():
                out_start(*ad, g)
                rows_out(g)

            @pl.when(g <= NB - 2)
            def _():
                cols_out(g + 1)

            @pl.when(g <= NB - 3)
            def _():
                finish(g + 2)

            return 0

        lax.fori_loop(0, NB + 1, step, 0)
        cols_out(0)
        finish(1)
        finish(0)

        def drain(c, _):
            for side in range(2):
                col_copy(side, c).wait_send()
                row_copy(side, c).wait_send()
                back_rows(side, c).wait_send()
                back_cols(side, c).wait_send()

            @pl.when(c != z)
            def _():
                for i in range(2):
                    out_copy(*ad, i, c).wait_send()
                    out_copy(*fin, i, c).wait_send()

            return 0

        lax.fori_loop(0, NB, drain, 0)

    for slot, offset in enumerate(OFFSETS[:-1]):
        t = lax.rem(z + offset + NB, NB)

        @pl.when(busy(t))
        def _():
            for i in range(4):
                z_copy(i, slot, t).wait_send()

    for outs, _, _, recv in (ad, fin):
        for h in range(HEADS):
            for i in range(2):
                arrived(outs[i].at[:, h * DH : (h + 1) * DH], recv.at[i, h])


def packed(array):
    frames, tile_h, tile_w, width = array.shape[1:]
    return jnp.transpose(array[0], (0, 2, 1, 3)).reshape(frames, tile_h * tile_w, width)


def unpacked(array):
    width = array.shape[-1]
    return jnp.transpose(array.reshape(FR, TW, TH, width), (0, 2, 1, 3))[None]


def shards(queries, cache_keys, cache_values, grad_attended, radius, frame_count):
    smem = pl.BlockSpec(memory_space=pltpu.SMEM)
    anywhere = pl.BlockSpec(memory_space=pl.ANY)
    dma = pltpu.SemaphoreType.DMA
    flat = jax.ShapeDtypeStruct((BLOCK, HEADS * DH), BF)
    outs = pl.pallas_call(
        fused_kernel,
        out_shape=(flat,) * 4,
        in_specs=[smem] * 2 + [anywhere] * 4,
        out_specs=(anywhere,) * 4,
        scratch_shapes=[
            pltpu.VMEM((2, NB, FR, WIDE, DH), BF),
            pltpu.VMEM((2, NB, DH, KEYS), BF),
            pltpu.VMEM((2, NB * BLOCK, DH), BF),
            pltpu.VMEM((3, WIDE, GROUP), F32),
            pltpu.VMEM((2 * GROUP, 2 * DH), BF),
            pltpu.VMEM((NB, KEYS, GROUP), F32),
            pltpu.VMEM((NB, KEYS, GROUP), F32),
            pltpu.VMEM((NB, KEYS, 2 * DH), F32),
            pltpu.VMEM((2, 2, NB, FR, 32, DH), BF),
            pltpu.VMEM((2, NB * BLOCK, DH), BF),
            pltpu.VMEM((2, 2, NB, FR, 32, DH), BF),
            pltpu.VMEM((2, 2, NB, FR, 32, DH), BF),
            pltpu.VMEM((2, 2, NB, FR, 8, DH), BF),
            pltpu.VMEM((2, 2, NB, FR, 8, DH), BF),
            pltpu.VMEM((2, NB, BLOCK, DH), BF),
            dma((4, NB)),
            dma((4, NB)),
        ]
        + [dma((2, NB))] * 12,
        compiler_params=pltpu.CompilerParams(collective_id=0, has_side_effects=True),
        name="fused",
    )(
        radius,
        frame_count,
        packed(cache_keys),
        packed(cache_values),
        packed(queries).reshape(BLOCK, HEADS * DH),
        packed(grad_attended).reshape(BLOCK, HEADS * DH),
    )
    return tuple(unpacked(x) for x in outs)


def solution(mesh):
    tiled = P("span", None, "ha", "wa", None)
    return jax.shard_map(
        shards,
        mesh=mesh,
        in_specs=(tiled,) * 4 + (P(), P()),
        out_specs=(tiled,) * 4,
        check_vma=False,
    )
```

time: 124 us -> 107 us (0.86)
  Pallas kernels: 104 us -> 96.8 us
  local copies, waits for them, and re-layouts: 14.5 us -> 8.95 us
  other arithmetic: 3.4 us -> 0 us
    pallas_call x2 -> x1, Pallas kernels: 104 us -> 96.8 us  [shards(): pl.pallas_call(fused_kernel, out_shape=(flat,) * 4, in_specs=[smem] * 2 +...]
    reshape x4 -> x2, local copies, waits for them, and re-layouts: 5.76 us -> 1.48 us  [packed(): jnp.transpose(array[0], (0, 2, 1, 3))]
    reshape x4, local copies, waits for them, and re-layouts: 6.7 us -> 3.94 us  [unpacked(): return jnp.transpose(array.reshape(FR, TW, TH, width), (0, 2, 1, 3))[None]]
    select_n x2 -> x0, other arithmetic: 2.73 us -> none  [the longest x1 2 us: shards(): near = jnp.where((reach <= own_radius) & inside, 0.0, HIDE).astype(F32)]
    another operation x0 -> x2, local copies, waits for them, and re-layouts: none -> 2.46 us  [the longest x1 1.72 us: shards(): packed(queries).reshape(BLOCK, HEADS * DH)]
    dynamic_slice x1 -> x0, local copies, waits for them, and re-layouts: 1.3 us -> none  [shards(): own_radius = radius[jnp.minimum(head_at(z), HEADS - 1)]]
where the time goes in v2:
time: 107 us; the launch traced here: 106 us
  Pallas kernels  96.8 us (90%)
  local copies, waits for them, and re-layouts  8.95 us (8%)
    pallas_call x1, Pallas kernels, shards(): pl.pallas_call(fused_kernel, out_shape=(flat,) * 4, in_specs=[smem] * 2 +...  96.8 us
    reshape x4, local copies, waits for them, and re-layouts, unpacked(): return jnp.transpose(array.reshape(FR, TW, TH, width), (0, 2, 1, 3))[None]  3.94 us

profile of v2, /device:TPU:1, one launch (start us, length us, event | category | flops | bytes accessed | tf_op | source)
XLA Modules:
  0.0 106.4 jit_solution(14876381087167506156)
XLA Ops:
  0.6 0.0 copy-start
  0.6 1.7 %reshape_reshape.6.q_in = bf16[144,768]{1,0:T(8,128)(2,1)} reshape(bf16[3,12,4,768]{3,2,1,0:T(4,128)(2,1)} %bitcast.24) | data formatting | bytes 442368 | tf_op jit(solution)/shard_map/reshape;reshape | solution.py:512
  2.4 0.0 copy-done
  2.4 0.0 copy-start.1
  2.4 0.7 reshape.26.k_in
  3.1 0.3 copy-done.1
  3.4 0.0 copy-start.2
  3.4 0.7 reshape.27.v_in
  4.1 0.3 copy-done.2
  4.4 0.7 reshape_reshape.7.g_in
  5.1 96.8 %fused.1 = (bf16[144,768]{1,0:T(8,128)(2,1)}, bf16[144,768]{1,0:T(8,128)(2,1)}, bf16[144,768]{1,0:T(8,128)(2,1)}, bf16[144,768]{1,0:T(8,128)(2,1)}) custom-call(s32[6]{0:T(128)} %radius.1, s32[8]{0:T(128)} %count.1, bf16[3,48,768]{2,1,0:T(8,128)(2,1)} %reshape.26.k_in, bf16[3,48,768]{2,1,0:T(8,128)(2,1)} %reshape.27.v_in, ...), custom_call_target="tpu_custom_call" | custom-call | tf_op jit(solution)/shard_map/fused/pallas_call | solution.py:480
  101.9 0.0 copy-start.5
  101.9 1.7 %reshape.28 = bf16[3,12,4,768]{3,2,1,0:T(4,128)(2,1)} reshape(bf16[144,768]{1,0:T(8,128)(2,1)} %get-tuple-element.8) | data formatting | bytes 442368 | tf_op jit(solution)/shard_map/reshape | solution.py:472
  103.7 0.0 copy-done.5
  103.7 0.0 copy-start.4
  103.7 0.7 reshape.29
  104.4 0.3 copy-done.4
  104.7 0.0 copy-start.3
  104.7 0.7 reshape.30
  105.4 0.3 copy-done.3
  105.7 0.7 reshape.31
Async XLA Ops:
  0.6 1.7 %copy-start = (bf16[1,3,4,12,768]{4,2,3,1,0:T(4,128)(2,1)S(1)}, bf16[1,3,4,12,768]{4,2,3,1,0:T(4,128)(2,1)}, u32[]{:S(2)}) copy-start(bf16[1,3,4,12,768]{4,2,3,1,0:T(4,128)(2,1)} %param.7) | copy-start | bytes 663556
  2.4 1.0 copy-start.1
  3.4 1.0 copy-start.2
  101.9 1.7 %copy-start.5 = (bf16[144,768]{1,0:T(8,128)(2,1)S(1)}, bf16[144,768]{1,0:T(8,128)(2,1)}, u32[]{:S(2)}) copy-start(bf16[144,768]{1,0:T(8,128)(2,1)} %get-tuple-element.9) | copy-start | bytes 663556
  103.7 1.0 copy-start.4
  104.7 1.0 copy-start.3

commit v3 on v2

--- a/solution.py
+++ b/solution.py
@@ -27,7 +27,10 @@
 HIDE = -1e30
 SCALE = 1.0 / math.sqrt(DH)
 LOG2E = math.log2(math.e)
-OFFSETS = (4, 3, -3, 2, -2, 1, -1, 0)
+STAGES = ((1, -1), (2, -2), (3, -3), (4,))
+OFFSETS = (1, -1, 2, -2, 3, -3, 4)
+KEYS_VALUES = (0, 1)
+QUERIES_GRADS = (2, 3)
 
 
 def place():
@@ -127,6 +130,8 @@
     dq_out,
     dk_out,
     dv_out,
+    wide,
+    asked,
     kv,
     kvt,
     qg,
@@ -169,25 +174,39 @@
 
     def target(i, c):
         if i < 2:
-            return kv.at[i, c, :, 0:OWN]
-        return qg.at[i - 2, block_rows(c)]
+            return wide.at[i, c, :, 0:TW]
+        return asked.at[i - 2, c]
 
     def source(i, t):
-        if i < 2:
-            return arrays[i].at[:, :, head_columns(head_at(t))]
-        return arrays[i].at[:, head_columns(head_at(t))]
-
-    def z_copy(i, slot, t):
+        return arrays[i].at[:, :, :, head_columns(head_at(t))]
+
+    def z_copy(i, offset, t):
+        slot = OFFSETS.index(offset)
         return remote(source(i, t), target(i, z), z_send.at[i, slot], z_recv.at[i, z], (t, a, w))
 
     def z_local(i):
         return pltpu.make_async_copy(source(i, z), target(i, z), z_recv.at[i, z])
 
+    def z_each(kinds, offsets, act):
+        for offset in offsets:
+            t = lax.rem(z + offset + NB, NB)
+
+            @pl.when(busy(t))
+            def _():
+                for i in kinds:
+                    act(z_copy(i, offset, t))
+
+    def z_start(kinds, offsets):
+        z_each(kinds, offsets, lambda copy: copy.start())
+
+    def z_sent(kinds, offsets):
+        z_each(kinds, offsets, lambda copy: copy.wait_send())
+
     def col_copy(side, c):
         if side == 0:
-            src, dst, to = kv.at[:, c, :, 0:8], kv.at[:, c, :, 56:64], shift_down(w, NW)
+            src, dst, to = wide.at[:, c, :, 0:2], wide.at[:, c, :, 14:16], shift_down(w, NW)
         else:
-            src, dst, to = kv.at[:, c, :, 40:48], kv.at[:, c, :, 48:56], shift_up(w, NW)
+            src, dst, to = wide.at[:, c, :, 10:12], wide.at[:, c, :, 12:14], shift_up(w, NW)
         return remote(src, dst, c_send.at[side, c], c_recv.at[side, c], (z, a, to))
 
     def row_copy(side, c):
@@ -199,17 +218,35 @@
             edge.at[side, :, c], dst, r_send.at[side, c], r_recv.at[side, c], (z, to, w)
         )
 
-    for kinds in ((0, 1), (2, 3)):
-        for slot, offset in enumerate(OFFSETS):
-            t = lax.rem(z + offset + NB, NB)
-
-            @pl.when(busy(t))
-            def _():
-                for i in kinds:
-                    if offset == 0:
-                        z_local(i).start()
-                    else:
-                        z_copy(i, slot, t).start()
+    early = z >= NB - 2
+
+    def first():
+        @pl.when(busy(z))
+        def _():
+            for i in range(4):
+                z_local(i).start()
+
+        @pl.when(early)
+        def _():
+            z_start(QUERIES_GRADS, OFFSETS)
+
+        z_start(KEYS_VALUES, STAGES[0])
+        z_start(KEYS_VALUES, STAGES[1])
+
+    def second():
+        z_sent(KEYS_VALUES, STAGES[0])
+        z_start(KEYS_VALUES, STAGES[2])
+
+    def third():
+        z_sent(KEYS_VALUES, STAGES[1])
+        z_start(KEYS_VALUES, STAGES[3])
+
+    def fourth():
+        z_sent(KEYS_VALUES, STAGES[2])
+
+        @pl.when(jnp.logical_not(early))
+        def _():
+            z_start(QUERIES_GRADS, OFFSETS)
 
     def gather():
         pick = picker((64, 64), 0)
@@ -225,7 +262,9 @@
                 col_copy(side, c).wait_recv()
             for i in range(2):
                 for f in range(FR):
-                    out = mm(pick, kv[i, c, f, 0:64, :]).astype(BF)
+                    tile = wide[i, c, f].reshape(64, DH)
+                    kv[i, c, f, 0:64, :] = tile
+                    out = mm(pick, tile).astype(BF)
                     edge[0, i, c, f] = out[0:32]
                     edge[1, i, c, f] = out[32:64]
             for side in range(2):
@@ -238,15 +277,29 @@
                 for f in range(FR):
                     kvt[i, c, :, f * WIDE : (f + 1) * WIDE] = kv[i, c, f].T
 
-        order = (0,) + OFFSETS[:-1]
-        blocks = [lax.rem(z + offset + NB, NB) for offset in order]
-        for n in range(NB + 2):
-            if n < NB:
-                cols_first(blocks[n])
-            if 1 <= n <= NB:
-                rows_next(blocks[n - 1])
+        steps = ((0,),) + STAGES
+        later = {1: second, 2: third, 3: fourth}
+        blocks = [[lax.rem(z + offset + NB, NB) for offset in step] for step in steps]
+        for n in range(len(steps) + 2):
+            if n < len(steps):
+                if n in later:
+                    later[n]()
+                for c in blocks[n]:
+                    cols_first(c)
+            if 1 <= n <= len(steps):
+                for c in blocks[n - 1]:
+                    rows_next(c)
             if n >= 2:
-                turn(blocks[n - 2])
+                for c in blocks[n - 2]:
+                    turn(c)
+
+    first()
+
+    @pl.when(jnp.logical_not(busy(z)))
+    def _():
+        second()
+        third()
+        fourth()
 
     def out_copy(outs, view, send, recv, i, c):
         return remote(
@@ -408,6 +461,7 @@
             def _():
                 for i in (2, 3):
                     arrived(target(i, g - 1), z_recv.at[i, g - 1])
+                    qg[i - 2, block_rows(g - 1), :] = asked[i - 2, g - 1].reshape(BLOCK, DH)
 
             compute(g)
 
@@ -448,13 +502,8 @@
 
         lax.fori_loop(0, NB, drain, 0)
 
-    for slot, offset in enumerate(OFFSETS[:-1]):
-        t = lax.rem(z + offset + NB, NB)
-
-        @pl.when(busy(t))
-        def _():
-            for i in range(4):
-                z_copy(i, slot, t).wait_send()
+    z_sent(KEYS_VALUES, STAGES[3])
+    z_sent(QUERIES_GRADS, OFFSETS)
 
     for outs, _, _, recv in (ad, fin):
         for h in range(HEADS):
@@ -462,14 +511,26 @@
                 arrived(outs[i].at[:, h * DH : (h + 1) * DH], recv.at[i, h])
 
 
-def packed(array):
-    frames, tile_h, tile_w, width = array.shape[1:]
-    return jnp.transpose(array[0], (0, 2, 1, 3)).reshape(frames, tile_h * tile_w, width)
-
-
-def unpacked(array):
-    width = array.shape[-1]
-    return jnp.transpose(array.reshape(FR, TW, TH, width), (0, 2, 1, 3))[None]
+def write_kernel(*refs):
+    flats, tiles, flat, tile, read, write = refs[:4], refs[4:8], *refs[8:]
+    reads = [pltpu.make_async_copy(flats[i], flat.at[i], read.at[i]) for i in range(4)]
+    writes = [pltpu.make_async_copy(tile.at[i], tiles[i], write.at[i]) for i in range(4)]
+    for copy in reads:
+        copy.start()
+    for i in range(4):
+        reads[i].wait()
+        tile[i] = flat[i].reshape(tile.shape[1:])
+        writes[i].start()
+    for copy in writes:
+        copy.wait()
+
+
+def by_columns(array):
+    return jnp.transpose(array[0], (0, 2, 1, 3))
+
+
+def by_rows(array):
+    return jnp.transpose(array, (0, 2, 1, 3))[None]
 
 
 def shards(queries, cache_keys, cache_values, grad_attended, radius, frame_count):
@@ -483,6 +544,8 @@
         in_specs=[smem] * 2 + [anywhere] * 4,
         out_specs=(anywhere,) * 4,
         scratch_shapes=[
+            pltpu.VMEM((2, NB, FR, 16, TH, DH), BF),
+            pltpu.VMEM((2, NB, FR, TW, TH, DH), BF),
             pltpu.VMEM((2, NB, FR, WIDE, DH), BF),
             pltpu.VMEM((2, NB, DH, KEYS), BF),
             pltpu.VMEM((2, NB * BLOCK, DH), BF),
@@ -507,12 +570,26 @@
     )(
         radius,
         frame_count,
-        packed(cache_keys),
-        packed(cache_values),
-        packed(queries).reshape(BLOCK, HEADS * DH),
-        packed(grad_attended).reshape(BLOCK, HEADS * DH),
+        by_columns(cache_keys),
+        by_columns(cache_values),
+        by_columns(queries),
+        by_columns(grad_attended),
     )
-    return tuple(unpacked(x) for x in outs)
+    tiles = (FR, TW, TH, HEADS * DH)
+    outs = pl.pallas_call(
+        write_kernel,
+        out_shape=(jax.ShapeDtypeStruct(tiles, BF),) * 4,
+        in_specs=[anywhere] * 4,
+        out_specs=(anywhere,) * 4,
+        scratch_shapes=[
+            pltpu.VMEM((4, BLOCK, HEADS * DH), BF),
+            pltpu.VMEM((4,) + tiles, BF),
+            dma((4,)),
+            dma((4,)),
+        ],
+        name="write",
+    )(*outs)
+    return tuple(by_rows(x) for x in outs)
 
 
 def solution(mesh):

time: 107 us -> 97.1 us (0.907)
  local copies, waits for them, and re-layouts: 8.95 us -> 0 us
  Pallas kernels: 96.8 us -> 95.6 us
    reshape x6 -> x0, local copies, waits for them, and re-layouts: 5.42 us -> none  [the longest x4 3.94 us: unpacked(): return jnp.transpose(array.reshape(FR, TW, TH, width), (0, 2, 1, 3))[None]]
    pallas_call x1, Pallas kernels: 96.8 us -> 93.5 us  [shards(): pl.pallas_call(fused_kernel, out_shape=(flat,) * 4, in_specs=[smem] * 2 +...]
    another operation x2 -> x0, local copies, waits for them, and re-layouts: 2.46 us -> none  [the longest x1 1.72 us: shards(): packed(queries).reshape(BLOCK, HEADS * DH)]
    pallas_call x0 -> x1, Pallas kernels: none -> 2.05 us  [shards(): pl.pallas_call(write_kernel, out_shape=(jax.ShapeDtypeStruct(tiles, BF),)...]
    unnamed x12 -> x0, local copies, waits for them, and re-layouts: 1.07 us -> none
where the time goes in v3:
time: 97.1 us; the launch traced here: 96.2 us
  Pallas kernels  95.6 us (98%)
    pallas_call x1, Pallas kernels, shards(): pl.pallas_call(fused_kernel, out_shape=(flat,) * 4, in_specs=[smem] * 2 +...  93.5 us
    pallas_call x1, Pallas kernels, shards(): pl.pallas_call(write_kernel, out_shape=(jax.ShapeDtypeStruct(tiles, BF),)...  2.05 us

profile of v3, /device:TPU:1, one launch (start us, length us, event | category | flops | bytes accessed | tf_op | source)
XLA Modules:
  0.0 96.2 jit_solution(13747039965848868017)
XLA Ops:
  0.6 93.5 %fused.1 = (bf16[144,768]{1,0:T(8,128)(2,1)}, bf16[144,768]{1,0:T(8,128)(2,1)}, bf16[144,768]{1,0:T(8,128)(2,1)}, bf16[144,768]{1,0:T(8,128)(2,1)}) custom-call(s32[6]{0:T(128)} %radius.1, s32[8]{0:T(128)} %count.1, bf16[3,12,4,768]{3,2,1,0:T(4,128)(2,1)} %bitcast.24, bf16[3,12,4,768]{3,2,1,0:T(4,128)(2,1)} %bitcast.25, bf16[3,12,4,768]{3,2,1,0:T(4,128)(2,1)} %bitcast.26, ...), custom_call_target="tpu_custom_call" | custom-call | tf_op jit(solution)/shard_map/fused/pallas_call | solution.py:541
  94.2 2.0 %write.1 = (bf16[3,12,4,768]{3,2,1,0:T(4,128)(2,1)}, bf16[3,12,4,768]{3,2,1,0:T(4,128)(2,1)}, bf16[3,12,4,768]{3,2,1,0:T(4,128)(2,1)}, bf16[3,12,4,768]{3,2,1,0:T(4,128)(2,1)}) custom-call(bf16[144,768]{1,0:T(8,128)(2,1)} %get-tuple-element.12.refs_0_, bf16[144,768]{1,0:T(8,128)(2,1)} %get-tuple-element.13.refs_1_, ...), custom_call_target="tpu_custom_call" | custom-call | tf_op jit(solution)/shard_map/write/pallas_call | solution.py:579

commit v4 on v3

--- a/solution.py
+++ b/solution.py
@@ -218,7 +218,7 @@
             edge.at[side, :, c], dst, r_send.at[side, c], r_recv.at[side, c], (z, to, w)
         )
 
-    early = z >= NB - 2
+    early = z >= NB
 
     def first():
         @pl.when(busy(z))
@@ -275,7 +275,7 @@
                 row_copy(side, c).wait_recv()
             for i in range(2):
                 for f in range(FR):
-                    kvt[i, c, :, f * WIDE : (f + 1) * WIDE] = kv[i, c, f].T
+                    kvt[i, c // 2, :, pl.ds(pl.multiple_of(lax.rem(c, 2) * KEYS + f * WIDE, WIDE), WIDE)] = kv[i, c, f].T
 
         steps = ((0,),) + STAGES
         later = {1: second, 2: third, 3: fourth}
@@ -353,13 +353,14 @@
         upstream = qg[1, rows, :]
         pair[0:GROUP, 0:DH] = qg[0, rows, :]
         pair[GROUP : 2 * GROUP, DH : 2 * DH] = upstream
-        chunks = jnp.minimum(g, NB - 1) + 1
+        chunks = jnp.minimum(g, NB - 1) // 2 + 1
         lane = lax.broadcasted_iota(jnp.int32, (1, GROUP), 1)
         pattern = lax.rem(g, 3)
 
         def both(j):
+            duo = pl.ds(2 * j, 2)
             return jnp.concatenate(
-                [kv[0, j].reshape(KEYS, DH), kv[1, j].reshape(KEYS, DH)], axis=1
+                [kv[0, duo].reshape(2 * KEYS, DH), kv[1, duo].reshape(2 * KEYS, DH)], axis=1
             )
 
         def folded(x, op):
@@ -367,14 +368,16 @@
 
         def score_step(j, top):
             r = nt(both(j), pair[...])
-            causal = jnp.where(lane + (g * GROUP - j * BLOCK) >= 0, 0.0, HIDE).astype(F32)
-            live = count[j]
-            for f in range(FR):
-                hidden = causal + jnp.where(f < live, 0.0, HIDE).astype(F32)
-                part = slice(f * WIDE, (f + 1) * WIDE)
-                s = r[part, 0:GROUP] + (near[pattern] + hidden)
-                scores[j, part, :] = s
-                top = jnp.maximum(top, folded(s, jnp.max))
+            for b in range(2):
+                block = 2 * j + b
+                causal = jnp.where(lane + (g * GROUP - block * BLOCK) >= 0, 0.0, HIDE).astype(F32)
+                live = count[block]
+                for f in range(FR):
+                    hidden = causal + jnp.where(f < live, 0.0, HIDE).astype(F32)
+                    part = slice((b * FR + f) * WIDE, (b * FR + f + 1) * WIDE)
+                    s = r[part, 0:GROUP] + (near[pattern] + hidden)
+                    scores[j, part, :] = s
+                    top = jnp.maximum(top, folded(s, jnp.max))
             pushes[j] = r[:, GROUP:]
             return top
 
@@ -411,12 +414,15 @@
     def part_of(i):
         return slice(i * DH, (i + 1) * DH)
 
+    def spot(at, low, high):
+        return pl.ds(pl.multiple_of(at + low, 8), high - low)
+
     def rows_out(c):
         for i in range(2):
             for f in range(FR):
-                at = f * WIDE
-                row_stage[0, i, c, f] = acc[c, at + 64 : at + 96, part_of(i)].astype(BF)
-                row_stage[1, i, c, f] = acc[c, at + 96 : at + 128, part_of(i)].astype(BF)
+                at = lax.rem(c, 2) * KEYS + f * WIDE
+                row_stage[0, i, c, f] = acc[c // 2, spot(at, 64, 96), part_of(i)].astype(BF)
+                row_stage[1, i, c, f] = acc[c // 2, spot(at, 96, 128), part_of(i)].astype(BF)
         for side in range(2):
             back_rows(side, c).start()
 
@@ -426,11 +432,11 @@
             back_rows(side, c).wait_recv()
         for i in range(2):
             for f in range(FR):
-                at = f * WIDE
+                at = lax.rem(c, 2) * KEYS + f * WIDE
                 border = jnp.concatenate([row_in[1, i, c, f], row_in[0, i, c, f]], axis=0)
-                acc[c, at : at + 64, part_of(i)] += mm(spread, border)
-                col_stage[0, i, c, f] = acc[c, at + 48 : at + 56, part_of(i)].astype(BF)
-                col_stage[1, i, c, f] = acc[c, at + 56 : at + 64, part_of(i)].astype(BF)
+                acc[c // 2, spot(at, 0, 64), part_of(i)] += mm(spread, border)
+                col_stage[0, i, c, f] = acc[c // 2, spot(at, 48, 56), part_of(i)].astype(BF)
+                col_stage[1, i, c, f] = acc[c // 2, spot(at, 56, 64), part_of(i)].astype(BF)
         for side in range(2):
             back_cols(side, c).start()
 
@@ -440,7 +446,7 @@
         for i in range(2):
             factor = SCALE if i == 0 else 1.0
             for f in range(FR):
-                whole = acc[c, f * WIDE : f * WIDE + OWN, part_of(i)]
+                whole = acc[c // 2, spot(lax.rem(c, 2) * KEYS + f * WIDE, 0, OWN), part_of(i)]
                 left = whole[0:8] + col_in[1, i, c, f].astype(F32)
                 right = whole[40:48] + col_in[0, i, c, f].astype(F32)
                 whole = jnp.concatenate([left, whole[8:40], right], axis=0)
@@ -547,13 +553,13 @@
             pltpu.VMEM((2, NB, FR, 16, TH, DH), BF),
             pltpu.VMEM((2, NB, FR, TW, TH, DH), BF),
             pltpu.VMEM((2, NB, FR, WIDE, DH), BF),
-            pltpu.VMEM((2, NB, DH, KEYS), BF),
+            pltpu.VMEM((2, NB // 2, DH, 2 * KEYS), BF),
             pltpu.VMEM((2, NB * BLOCK, DH), BF),
             pltpu.VMEM((3, WIDE, GROUP), F32),
             pltpu.VMEM((2 * GROUP, 2 * DH), BF),
-            pltpu.VMEM((NB, KEYS, GROUP), F32),
-            pltpu.VMEM((NB, KEYS, GROUP), F32),
-            pltpu.VMEM((NB, KEYS, 2 * DH), F32),
+            pltpu.VMEM((NB // 2, 2 * KEYS, GROUP), F32),
+            pltpu.VMEM((NB // 2, 2 * KEYS, GROUP), F32),
+            pltpu.VMEM((NB // 2, 2 * KEYS, 2 * DH), F32),
             pltpu.VMEM((2, 2, NB, FR, 32, DH), BF),
             pltpu.VMEM((2, NB * BLOCK, DH), BF),
             pltpu.VMEM((2, 2, NB, FR, 32, DH), BF),

time: 97.1 us -> 85.4 us (0.88)
  Pallas kernels: 95.6 us -> 83.1 us
    pallas_call x1, Pallas kernels: 93.5 us -> 81.1 us  [shards(): pl.pallas_call(fused_kernel, out_shape=(flat,) * 4, in_specs=[smem] * 2 +...]
where the time goes in v4:
time: 85.4 us; the launch traced here: 83.8 us
  Pallas kernels  83.1 us (97%)
    pallas_call x1, Pallas kernels, shards(): pl.pallas_call(fused_kernel, out_shape=(flat,) * 4, in_specs=[smem] * 2 +...  81.1 us
    pallas_call x1, Pallas kernels, shards(): pl.pallas_call(write_kernel, out_shape=(jax.ShapeDtypeStruct(tiles, BF),)...  2.05 us

profile of v4, /device:TPU:1, one launch (start us, length us, event | category | flops | bytes accessed | tf_op | source)
XLA Modules:
  0.0 83.8 jit_solution(11693519493037547739)
XLA Ops:
  0.6 81.1 %fused.1 = (bf16[144,768]{1,0:T(8,128)(2,1)}, bf16[144,768]{1,0:T(8,128)(2,1)}, bf16[144,768]{1,0:T(8,128)(2,1)}, bf16[144,768]{1,0:T(8,128)(2,1)}) custom-call(s32[6]{0:T(128)} %radius.1, s32[8]{0:T(128)} %count.1, bf16[3,12,4,768]{3,2,1,0:T(4,128)(2,1)} %bitcast.24, bf16[3,12,4,768]{3,2,1,0:T(4,128)(2,1)} %bitcast.25, bf16[3,12,4,768]{3,2,1,0:T(4,128)(2,1)} %bitcast.26, ...), custom_call_target="tpu_custom_call" | custom-call | tf_op jit(solution)/shard_map/fused/pallas_call | solution.py:547
  81.7 2.0 %write.1 = (bf16[3,12,4,768]{3,2,1,0:T(4,128)(2,1)}, bf16[3,12,4,768]{3,2,1,0:T(4,128)(2,1)}, bf16[3,12,4,768]{3,2,1,0:T(4,128)(2,1)}, bf16[3,12,4,768]{3,2,1,0:T(4,128)(2,1)}) custom-call(bf16[144,768]{1,0:T(8,128)(2,1)} %get-tuple-element.12.refs_0_, bf16[144,768]{1,0:T(8,128)(2,1)} %get-tuple-element.13.refs_1_, ...), custom_call_target="tpu_custom_call" | custom-call | tf_op jit(solution)/shard_map/write/pallas_call | solution.py:585

commit v5 on v4

--- a/solution.py
+++ b/solution.py
@@ -27,7 +27,7 @@
 HIDE = -1e30
 SCALE = 1.0 / math.sqrt(DH)
 LOG2E = math.log2(math.e)
-STAGES = ((1, -1), (2, -2), (3, -3), (4,))
+STAGES = ((4, 1, -1), (3, -3), (2, -2), ())
 OFFSETS = (1, -1, 2, -2, 3, -3, 4)
 KEYS_VALUES = (0, 1)
 QUERIES_GRADS = (2, 3)
@@ -218,7 +218,7 @@
             edge.at[side, :, c], dst, r_send.at[side, c], r_recv.at[side, c], (z, to, w)
         )
 
-    early = z >= NB
+    upper = z >= NB // 2
 
     def first():
         @pl.when(busy(z))
@@ -226,10 +226,6 @@
             for i in range(4):
                 z_local(i).start()
 
-        @pl.when(early)
-        def _():
-            z_start(QUERIES_GRADS, OFFSETS)
-
         z_start(KEYS_VALUES, STAGES[0])
         z_start(KEYS_VALUES, STAGES[1])
 
@@ -244,7 +240,12 @@
     def fourth():
         z_sent(KEYS_VALUES, STAGES[2])
 
-        @pl.when(jnp.logical_not(early))
+        @pl.when(upper)
+        def _():
+            z_start(QUERIES_GRADS, OFFSETS)
+
+    def fifth():
+        @pl.when(jnp.logical_not(upper))
         def _():
             z_start(QUERIES_GRADS, OFFSETS)
 
@@ -300,6 +301,8 @@
         second()
         third()
         fourth()
+        z_sent(KEYS_VALUES, STAGES[3])
+        fifth()
 
     def out_copy(outs, view, send, recv, i, c):
         return remote(
@@ -459,6 +462,8 @@
         pair[...] = jnp.zeros_like(pair)
         acc[...] = jnp.zeros_like(acc)
         gather()
+        z_sent(KEYS_VALUES, STAGES[3])
+        fifth()
 
         def step(n, _):
             g = NB - n
@@ -508,7 +513,6 @@
 
         lax.fori_loop(0, NB, drain, 0)
 
-    z_sent(KEYS_VALUES, STAGES[3])
     z_sent(QUERIES_GRADS, OFFSETS)
 
     for outs, _, _, recv in (ad, fin):

time: 85.4 us -> 82.1 us (0.961); the launches traced: 83.8 us -> 81.9 us
  Pallas kernels: 83.1 us -> 81.2 us
    pallas_call x1, Pallas kernels: 81.1 us -> 79.2 us  [shards(): pl.pallas_call(fused_kernel, out_shape=(flat,) * 4, in_specs=[smem] * 2 +...]
where the time goes in v5:
time: 82.1 us; the launch traced here: 81.9 us
  Pallas kernels  81.2 us (99%)
    pallas_call x1, Pallas kernels, shards(): pl.pallas_call(fused_kernel, out_shape=(flat,) * 4, in_specs=[smem] * 2 +...  79.2 us
    pallas_call x1, Pallas kernels, shards(): pl.pallas_call(write_kernel, out_shape=(jax.ShapeDtypeStruct(tiles, BF),)...  2.05 us

profile of v5, /device:TPU:1, one launch (start us, length us, event | category | flops | bytes accessed | tf_op | source)
XLA Modules:
  0.0 81.9 jit_solution(11564518745199692577)
XLA Ops:
  0.6 79.2 %fused.1 = (bf16[144,768]{1,0:T(8,128)(2,1)}, bf16[144,768]{1,0:T(8,128)(2,1)}, bf16[144,768]{1,0:T(8,128)(2,1)}, bf16[144,768]{1,0:T(8,128)(2,1)}) custom-call(s32[6]{0:T(128)} %radius.1, s32[8]{0:T(128)} %count.1, bf16[3,12,4,768]{3,2,1,0:T(4,128)(2,1)} %bitcast.24, bf16[3,12,4,768]{3,2,1,0:T(4,128)(2,1)} %bitcast.25, bf16[3,12,4,768]{3,2,1,0:T(4,128)(2,1)} %bitcast.26, ...), custom_call_target="tpu_custom_call" | custom-call | tf_op jit(solution)/shard_map/fused/pallas_call | solution.py:551
  79.8 2.0 %write.1 = (bf16[3,12,4,768]{3,2,1,0:T(4,128)(2,1)}, bf16[3,12,4,768]{3,2,1,0:T(4,128)(2,1)}, bf16[3,12,4,768]{3,2,1,0:T(4,128)(2,1)}, bf16[3,12,4,768]{3,2,1,0:T(4,128)(2,1)}) custom-call(bf16[144,768]{1,0:T(8,128)(2,1)} %get-tuple-element.12.refs_0_, bf16[144,768]{1,0:T(8,128)(2,1)} %get-tuple-element.13.refs_1_, ...), custom_call_target="tpu_custom_call" | custom-call | tf_op jit(solution)/shard_map/write/pallas_call | solution.py:589

commit v6 on v5

--- a/solution.py
+++ b/solution.py
@@ -309,17 +309,17 @@
             view(i, c), outs[i].at[:, head_columns(me)], send.at[i, c], recv.at[i, me], (c, a, w)
         )
 
-    def out_start(outs, view, send, recv, c):
+    def out_start(outs, view, send, recv, c, kinds=(0, 1)):
         @pl.when(c == z)
         def _():
-            for i in range(2):
+            for i in kinds:
                 pltpu.make_async_copy(
                     view(i, c), outs[i].at[:, head_columns(me)], recv.at[i, me]
                 ).start()
 
         @pl.when(c != z)
         def _():
-            for i in range(2):
+            for i in kinds:
                 out_copy(outs, view, send, recv, i, c).start()
 
     def ad_view(i, c):
@@ -360,17 +360,12 @@
         lane = lax.broadcasted_iota(jnp.int32, (1, GROUP), 1)
         pattern = lax.rem(g, 3)
 
-        def both(j):
-            duo = pl.ds(2 * j, 2)
-            return jnp.concatenate(
-                [kv[0, duo].reshape(2 * KEYS, DH), kv[1, duo].reshape(2 * KEYS, DH)], axis=1
-            )
-
         def folded(x, op):
             return op(x.reshape(x.shape[0] // 8, 8, GROUP), axis=0)
 
         def score_step(j, top):
-            r = nt(both(j), pair[...])
+            duo = pl.ds(2 * j, 2)
+            r = nt(kv[0, duo].reshape(2 * KEYS, DH), pair[0:GROUP, 0:DH])
             for b in range(2):
                 block = 2 * j + b
                 causal = jnp.where(lane + (g * GROUP - block * BLOCK) >= 0, 0.0, HIDE).astype(F32)
@@ -378,10 +373,10 @@
                 for f in range(FR):
                     hidden = causal + jnp.where(f < live, 0.0, HIDE).astype(F32)
                     part = slice((b * FR + f) * WIDE, (b * FR + f + 1) * WIDE)
-                    s = r[part, 0:GROUP] + (near[pattern] + hidden)
+                    s = r[part, :] + (near[pattern] + hidden)
                     scores[j, part, :] = s
                     top = jnp.maximum(top, folded(s, jnp.max))
-            pushes[j] = r[:, GROUP:]
+            pushes[j] = nt(kv[1, duo].reshape(2 * KEYS, DH), pair[GROUP:, DH:])
             return top
 
         top = lax.fori_loop(0, chunks, score_step, jnp.full((8, GROUP), HIDE, F32))
@@ -405,10 +400,16 @@
         ad_stage[0, rows, :] = attended.T
         inverse = 1.0 / total
 
+        @pl.when(g <= NB - 1)
+        def _():
+            out_start(*ad, g, (0,))
+
+
         def grad_step(j, grad_q):
             prob = scores[j] * inverse
             slope = (prob * (pushes[j] - delta)).astype(BF)
-            acc[j] += mm(jnp.concatenate([slope, prob.astype(BF)], axis=1), pair[...])
+            acc[j, :, 0:DH] += mm(slope, pair[0:GROUP, 0:DH])
+            acc[j, :, DH:] += mm(prob.astype(BF), pair[GROUP:, DH:])
             return grad_q + mm(kvt[0, j], slope)
 
         grad_q = lax.fori_loop(0, chunks, grad_step, zero)
@@ -478,7 +479,7 @@
 
             @pl.when(g <= NB - 1)
             def _():
-                out_start(*ad, g)
+                out_start(*ad, g, (1,))
                 rows_out(g)
 
             @pl.when(g <= NB - 2)

time: 82.1 us -> 80.9 us (0.985)
  Pallas kernels: 81.2 us -> 79.7 us
    pallas_call x1, Pallas kernels: 79.2 us -> 77.6 us  [shards(): pl.pallas_call(fused_kernel, out_shape=(flat,) * 4, in_specs=[smem] * 2 +...]
where the time goes in v6:
time: 80.9 us; the launch traced here: 80.3 us
  Pallas kernels  79.7 us (99%)
    pallas_call x1, Pallas kernels, shards(): pl.pallas_call(fused_kernel, out_shape=(flat,) * 4, in_specs=[smem] * 2 +...  77.6 us
    pallas_call x1, Pallas kernels, shards(): pl.pallas_call(write_kernel, out_shape=(jax.ShapeDtypeStruct(tiles, BF),)...  2.05 us

profile of v6, /device:TPU:1, one launch (start us, length us, event | category | flops | bytes accessed | tf_op | source)
XLA Modules:
  0.0 80.3 jit_solution(17224450055751863747)
XLA Ops:
  0.6 77.6 %fused.1 = (bf16[144,768]{1,0:T(8,128)(2,1)}, bf16[144,768]{1,0:T(8,128)(2,1)}, bf16[144,768]{1,0:T(8,128)(2,1)}, bf16[144,768]{1,0:T(8,128)(2,1)}) custom-call(s32[6]{0:T(128)} %radius.1, s32[8]{0:T(128)} %count.1, bf16[3,12,4,768]{3,2,1,0:T(4,128)(2,1)} %bitcast.24, bf16[3,12,4,768]{3,2,1,0:T(4,128)(2,1)} %bitcast.25, bf16[3,12,4,768]{3,2,1,0:T(4,128)(2,1)} %bitcast.26, ...), custom_call_target="tpu_custom_call" | custom-call | tf_op jit(solution)/shard_map/fused/pallas_call | solution.py:552
  78.3 2.0 %write.1 = (bf16[3,12,4,768]{3,2,1,0:T(4,128)(2,1)}, bf16[3,12,4,768]{3,2,1,0:T(4,128)(2,1)}, bf16[3,12,4,768]{3,2,1,0:T(4,128)(2,1)}, bf16[3,12,4,768]{3,2,1,0:T(4,128)(2,1)}) custom-call(bf16[144,768]{1,0:T(8,128)(2,1)} %get-tuple-element.12.refs_0_, bf16[144,768]{1,0:T(8,128)(2,1)} %get-tuple-element.13.refs_1_, ...), custom_call_target="tpu_custom_call" | custom-call | tf_op jit(solution)/shard_map/write/pallas_call | solution.py:590

commit v7 on v6

--- a/solution.py
+++ b/solution.py
@@ -486,13 +486,14 @@
             def _():
                 cols_out(g + 1)
 
-            @pl.when(g <= NB - 3)
+            @pl.when(g <= NB - 4)
             def _():
-                finish(g + 2)
+                finish(g + 3)
 
             return 0
 
         lax.fori_loop(0, NB + 1, step, 0)
+        finish(2)
         cols_out(0)
         finish(1)
         finish(0)

time: 80.9 us -> 79.9 us (0.988)
  no operation moved by 1% of the time
where the time goes in v7:
time: 79.9 us; the launch traced here: 79.7 us
  Pallas kernels  79 us (99%)
    pallas_call x1, Pallas kernels, shards(): pl.pallas_call(fused_kernel, out_shape=(flat,) * 4, in_specs=[smem] * 2 +...  77 us
    pallas_call x1, Pallas kernels, shards(): pl.pallas_call(write_kernel, out_shape=(jax.ShapeDtypeStruct(tiles, BF),)...  2.05 us

profile of v7, /device:TPU:1, one launch (start us, length us, event | category | flops | bytes accessed | tf_op | source)
XLA Modules:
  0.0 79.7 jit_solution(16555757059720652700)
XLA Ops:
  0.6 77.0 %fused.1 = (bf16[144,768]{1,0:T(8,128)(2,1)}, bf16[144,768]{1,0:T(8,128)(2,1)}, bf16[144,768]{1,0:T(8,128)(2,1)}, bf16[144,768]{1,0:T(8,128)(2,1)}) custom-call(s32[6]{0:T(128)} %radius.1, s32[8]{0:T(128)} %count.1, bf16[3,12,4,768]{3,2,1,0:T(4,128)(2,1)} %bitcast.24, bf16[3,12,4,768]{3,2,1,0:T(4,128)(2,1)} %bitcast.25, bf16[3,12,4,768]{3,2,1,0:T(4,128)(2,1)} %bitcast.26, ...), custom_call_target="tpu_custom_call" | custom-call | tf_op jit(solution)/shard_map/fused/pallas_call | solution.py:553
  77.6 2.0 %write.1 = (bf16[3,12,4,768]{3,2,1,0:T(4,128)(2,1)}, bf16[3,12,4,768]{3,2,1,0:T(4,128)(2,1)}, bf16[3,12,4,768]{3,2,1,0:T(4,128)(2,1)}, bf16[3,12,4,768]{3,2,1,0:T(4,128)(2,1)}) custom-call(bf16[144,768]{1,0:T(8,128)(2,1)} %get-tuple-element.12.refs_0_, bf16[144,768]{1,0:T(8,128)(2,1)} %get-tuple-element.13.refs_1_, ...), custom_call_target="tpu_custom_call" | custom-call | tf_op jit(solution)/shard_map/write/pallas_call | solution.py:591
